TPU v7x, 32 devices: a whole 2x2x4 slice. The times are simulated.
32 devices in a mesh: req: 4 (over x, core), exp: 8 (over z, y).
Axes of the slice: x: 2, y: 2, z: 4, core: 2. Of those that a mesh axis runs over, the one named last changes fastest.
Arguments:
- query: bfloat16 [2048, 2048], P(('req', 'exp'))
- new_kv: bfloat16 [2048, 1024], P(('req', 'exp')), may hold values from -6 to 6
- cache_kv: bfloat16 [4, 2048, 1024], P('req', 'exp')
- cached_len: int32 [4], replicated, may hold values from 0 to 2048, as said below
- residual: bfloat16 [2048, 2048], P(('req', 'exp')), may hold values from -6 to 6
- w_out: bfloat16 [2048, 2048], replicated, may hold values from -4 to 4
- gain: float32 [2048], replicated, may hold values from 0.1 to 1.9
- routes: int32 [2048, 6], P(('req', 'exp')), may hold values from 0 to 63, all different within a row; in each aligned block of 64 rows (0 to 63, 64 to 127, ...) at most 7 rows name the same one
- gates: bfloat16 [2048, 6], P(('req', 'exp')), may hold values from 0.049804688 to 0.59765625
- w_gate: bfloat16 [128, 2048, 704], P(('req', 'exp')), may hold values from -0.125 to 0.125
- w_up: bfloat16 [128, 2048, 704], P(('req', 'exp')), may hold values from -0.125 to 0.125
- w_down: bfloat16 [128, 704, 2048], P(('req', 'exp')), may hold values from -0.3125 to 0.3125
Outputs:
- output: bfloat16 [2048, 2048], P(('req', 'exp'))
Inputs may be any that keep to these rules, and one draw needn't show every extreme that they name: `routes`: in the 64 rows of one device no expert is named by more than 7 rows, a bound that some block reaches; a row names 6 different experts. `cached_len`: the largest is exactly 2048, and 1 requests have none.
All inputs are finite; a program needn't handle non-finite values.
Results may differ from a plain program's by a relative error of at most 0.033.
Values may be sent and summed in bfloat16 or wider, within the bound.
A program may use at most 128 MiB of HBM per device.

v0:
```python
import math

import jax
import jax.numpy as jnp
from jax import lax
from jax.sharding import PartitionSpec as P

D = 2048
H = 16
KVH = 4
HD = 128
EXPERTS = 64
TOPK = 6
HALVES = 2
CAP = 7


def visibility(key_row, key_device, query_index, lens_group, piece_len, tok_rows, new_len):
    req_here = lens_group.shape[0]
    cache_rows = req_here * piece_len
    is_cache = key_row < cache_rows
    cache_req = key_row // piece_len
    cache_pos = key_device * piece_len + key_row % piece_len
    new_token = key_device * tok_rows + key_row - cache_rows
    key_req = jnp.where(is_cache, cache_req, new_token // new_len)
    key_pos = new_token % new_len
    owners = jnp.arange(req_here, dtype=jnp.int32)
    cache_len = jnp.sum(
        jnp.where(cache_req[:, None] == owners[None, :], lens_group[None, :], 0), axis=1
    )
    query_req = query_index // new_len
    query_pos = query_index % new_len
    same = key_req[None, :] == query_req[:, None]
    seen = jnp.where(
        is_cache[None, :], (cache_pos < cache_len)[None, :], key_pos[None, :] <= query_pos[:, None]
    )
    return same & seen


def head_scores(queries, keys):
    count = queries.shape[0]
    qh = queries.reshape(count, KVH, H // KVH, HD)
    kh = keys.reshape(keys.shape[0], KVH, HD)
    return jnp.einsum("qgjd,kgd->qgjk", qh, kh, preferred_element_type=jnp.float32) * (
        1.0 / math.sqrt(HD)
    )


def weighted_values(weights, values):
    vh = values.reshape(values.shape[0], KVH, HD)
    return jnp.einsum("qgjk,kgd->qgjd", weights, vh, preferred_element_type=jnp.float32)


def shards(
    query, new_kv, cache_kv, cached_len, residual, w_out, gain, routes, gates, w_gate, w_up, w_down
):
    tok_rows = query.shape[0]
    n_exp = lax.axis_size("exp")
    n_req = lax.axis_size("req")
    req_here = cache_kv.shape[0]
    piece_len = cache_kv.shape[1]
    kv_cols = cache_kv.shape[2] // 2
    new_len = tok_rows * n_exp // req_here
    group_index = lax.axis_index("req")
    column = lax.axis_index("exp")
    lens_group = lax.dynamic_slice_in_dim(cached_len, group_index * req_here, req_here)
    keys_local = jnp.concatenate([cache_kv.reshape(req_here * piece_len, 2 * kv_cols), new_kv], 0)
    block_rows = keys_local.shape[0]
    q_all = lax.all_gather(query, "exp", axis=0, tiled=True)
    count = q_all.shape[0]
    seen = visibility(
        jnp.arange(block_rows, dtype=jnp.int32),
        column,
        jnp.arange(count, dtype=jnp.int32),
        lens_group,
        piece_len,
        tok_rows,
        new_len,
    )
    scores = head_scores(q_all, keys_local[:, :kv_cols])
    masked = jnp.where(seen[:, None, None, :], scores, -1e30)
    peak = jnp.max(masked, axis=-1)
    expo = jnp.where(seen[:, None, None, :], jnp.exp(masked - peak[..., None]), 0.0)
    total = jnp.sum(expo, axis=-1)
    partial_value = weighted_values(expo.astype(jnp.bfloat16), keys_local[:, kv_cols:]).reshape(
        count, H * HD
    )
    peaks, totals, partials = (
        lax.all_to_all(
            peak.reshape(count, H).astype(jnp.bfloat16),
            "exp",
            split_axis=0,
            concat_axis=0,
            tiled=True,
        ).astype(jnp.float32),
        lax.all_to_all(
            total.reshape(count, H).astype(jnp.bfloat16),
            "exp",
            split_axis=0,
            concat_axis=0,
            tiled=True,
        ).astype(jnp.float32),
        lax.all_to_all(
            partial_value.astype(jnp.bfloat16), "exp", split_axis=0, concat_axis=0, tiled=True
        ).astype(partial_value.dtype),
    )
    peaks = peaks.reshape(n_exp, tok_rows, H)
    totals = totals.reshape(n_exp, tok_rows, H)
    top = jnp.max(peaks, axis=0)
    factor = jnp.exp(peaks - top[None])
    denom = jnp.sum(factor * totals, axis=0)
    numer = jnp.sum(factor[..., None] * partials.reshape(n_exp, tok_rows, H, HD), axis=0)
    attended = (numer / denom[..., None]).reshape(tok_rows, H * HD).astype(jnp.bfloat16)
    stream = (
        residual.astype(jnp.float32) + jnp.dot(attended, w_out, preferred_element_type=jnp.float32)
    ).astype(jnp.bfloat16)
    wide = stream.astype(jnp.float32)
    normed = (
        wide * lax.rsqrt(jnp.mean(wide * wide, axis=-1, keepdims=True) + 1e-06) * gain
    ).astype(jnp.bfloat16)
    rows_here = w_gate.shape[0]
    devices = n_req * n_exp
    flat = routes.reshape(-1)
    hits = (flat[:, None] == jnp.arange(EXPERTS, dtype=jnp.int32)[None, :]).astype(jnp.int32)
    slot = jnp.sum(hits * (jnp.cumsum(hits, axis=0) - 1), axis=1)
    place = flat * CAP + slot
    width = EXPERTS * CAP
    chosen = (place[:, None] == jnp.arange(width, dtype=jnp.int32)[None, :]).reshape(
        tok_rows, TOPK, width
    )
    sender = jnp.sum(chosen.astype(jnp.float32), axis=1).astype(jnp.bfloat16)
    send = jnp.einsum("tp,td->pd", sender, normed, preferred_element_type=jnp.float32).astype(
        jnp.bfloat16
    )
    send = send.reshape(EXPERTS // rows_here, rows_here * CAP, D)
    spread = jnp.concatenate([send] * HALVES, 0)
    mixer = jnp.sum(jnp.where(chosen, gates.astype(jnp.float32)[:, :, None], 0.0), axis=1).astype(
        jnp.bfloat16
    )
    arrived = lax.all_to_all(spread, ("req", "exp"), split_axis=0, concat_axis=0, tiled=True)
    pieces = arrived.reshape(devices, rows_here, CAP, D)
    gate_v = jnp.einsum("srcd,rdf->srcf", pieces, w_gate, preferred_element_type=jnp.float32)
    up_v = jnp.einsum("srcd,rdf->srcf", pieces, w_up, preferred_element_type=jnp.float32)
    hidden = (jax.nn.silu(gate_v) * up_v).astype(jnp.bfloat16)
    result = jnp.einsum("srcf,rfd->srcd", hidden, w_down, preferred_element_type=jnp.float32)
    partial_out = result.astype(jnp.bfloat16).reshape(devices, rows_here * CAP, D)
    collected = lax.all_to_all(partial_out, ("req", "exp"), split_axis=0, concat_axis=0, tiled=True)
    back = jnp.sum(collected.reshape(HALVES, width, D).astype(jnp.float32), axis=0).astype(
        jnp.bfloat16
    )
    mixed = jnp.dot(mixer, back, preferred_element_type=jnp.float32)
    return (stream.astype(jnp.float32) + mixed).astype(jnp.bfloat16)


def solution(mesh):
    return jax.shard_map(
        shards,
        mesh=mesh,
        in_specs=(
            P(("req", "exp"), None),
            P(("req", "exp"), None),
            P("req", "exp", None),
            P(),
            P(("req", "exp"), None),
            P(),
            P(),
            P(("req", "exp"), None),
            P(("req", "exp"), None),
            P(("req", "exp"), None, None),
            P(("req", "exp"), None, None),
            P(("req", "exp"), None, None),
        ),
        out_specs=P(("req", "exp"), None),
        check_vma=False,
    )
```

profile of v0, /device:TPU:0, one launch (start us, length us, event | category | flops | bytes accessed | tf_op | source)
XLA Modules:
  0.0 412.1 jit_solution(14217930707333338113)
XLA Ops:
  6.5 0.7 all-gather.2.cloned.1.call-update
  7.3 1.2 pad_maximum_fusion.1
  8.6 1.2 dynamic_slice.3
  9.8 0.7 fusion.52
  10.5 0.3 select_and_fusion
  10.8 50.7 %all-gather.2.cloned.1.call-done = bf16[512,2048]{1,0:T(8,128)(2,1)} async-done(((bf16[64,2048]{1,0:T(8,128)(2,1)}), bf16[512,2048]{1,0:T(8,128)(2,1)}) %all-gather.2.cloned.1.call-update) | async-done | bytes 2097168 | tf_op jit(solution)/shard_map/all_gather | solution.py:69
  61.5 2.9 copy.82
  64.4 5.9 %fusion.6 = (f32[512,4,4]{0,2,1:T(4,128)S(1)}, f32[4,320,512,4]{2,1,3,0:T(8,128)}) fusion(pred[512,320]{0,1:T(8,128)(4,1)S(1)} %select_and_fusion, bf16[512,4,4,128]{0,3,2,1:T(8,128)(2,1)S(1)} %bitcast.114, bf16[320,4,128,1]{2,1,0,3:T(4,128)(2,1)S(1)} %bitcast.119), kind=kOutput, calls=%fused_computation.8 | convolution fusion | flops 678944768 | bytes 13107200 | tf_op jit(solution)/shard_map/qgjd,kgd->qgjk/dot_general | solution.py:44
  70.3 0.1 convert_element_type.92
  70.4 0.7 reshape.277
  71.1 3.3 all-to-all-start
  74.4 6.5 %fusion.7 = bf16[512,4,4]{0,2,1:T(4,128)(2,1)S(1)} fusion(f32[4,320,512,4]{2,1,3,0:T(8,128)} %get-tuple-element.12, f32[512,4,4]{0,2,1:T(4,128)S(1)} %get-tuple-element.11, pred[512,320]{0,1:T(8,128)(4,1)S(1)} %select_and_fusion), kind=kLoop, calls=%fused_computation.9 | loop fusion | flops 13099008 | bytes 10698752 | tf_op jit(solution)/shard_map/reduce_sum | solution.py:84
  81.1 0.7 reshape.279
  81.7 5.9 %all-to-all-start.2 = ((bf16[8,2,512]{2,1,0:T(2,128)(2,1)}), bf16[8,2,512]{2,1,0:T(2,128)(2,1)S(1)}, u32[]{:S(2)}, u32[]{:S(2)}) async-start(bf16[8,2,512]{2,1,0:T(2,128)(2,1)} %reshape.279), calls=%async_computation.2 | async-start | bytes 32768 | tf_op jit(solution)/shard_map/all_to_all | solution.py:96
  87.7 8.2 %convert_bitcast_fusion = bf16[512,4,4,128]{0,3,2,1:T(8,128)(2,1)} fusion(f32[4,320,512,4]{2,1,3,0:T(8,128)} %get-tuple-element.12, f32[512,4,4]{0,2,1:T(4,128)S(1)} %get-tuple-element.11, pred[512,320]{0,1:T(8,128)(4,1)S(1)} %select_and_fusion, bf16[320,4,128,1]{2,1,0,3:T(4,128)(2,1)S(1)} %bitcast.121), kind=kOutput, calls=%fused_computation.29 | convolution fusion | flops 685244416 | bytes 13107200 | tf_op jit(solution)/shard_map/qgjk,kgd->qgjd/dot_general | solution.py:51
  95.8 3.4 copy.88
  99.3 2.9 convert_element_type.97
  102.2 6.0 %all-to-all-start.1 = ((bf16[8,64,2048]{2,1,0:T(8,128)(2,1)}), bf16[8,64,2048]{2,1,0:T(8,128)(2,1)S(1)}, u32[]{:S(2)}, u32[]{:S(2)}) async-start(bf16[8,64,2048]{2,1,0:T(8,128)(2,1)} %convert_element_type.97), calls=%async_computation.1 | async-start | bytes 4194304 | tf_op jit(solution)/shard_map/all_to_all | solution.py:103
  108.2 0.1 copy.92
  108.3 0.1 eq.80
  108.4 0.1 eq.76
  108.6 0.9 reduce-window.6
  109.5 0.2 slice_reduce_fusion
  109.8 0.1 fusion.38
  109.9 0.1 reduce_sum.85
  110.1 0.2 select_reduce_fusion
  110.4 0.1 reshape.278
  110.5 0.1 reshape.280
  110.7 0.1 copy.86
  110.8 2.6 mul.73
  113.4 4.9 %mul.74 = f32[8,64,2048]{2,1,0:T(8,128)} reshape(f32[8,64,16,128]{3,2,1,0:T(8,128)} %mul.73) | data formatting | bytes 8388608 | tf_op jit(solution)/shard_map/mul | solution.py:112
  118.3 36.7 %all-to-all-done.1 = bf16[8,64,2048]{2,1,0:T(8,128)(2,1)S(1)} async-done(((bf16[8,64,2048]{2,1,0:T(8,128)(2,1)}), bf16[8,64,2048]{2,1,0:T(8,128)(2,1)S(1)}, u32[]{:S(2)}, u32[]{:S(2)}) %all-to-all-start.1) | async-done | bytes 2097184 | tf_op jit(solution)/shard_map/all_to_all | solution.py:103
  155.0 2.8 multiply_reduce_fusion
  157.9 0.2 div.57
  158.1 5.2 %multiply_reduce_fusion.1 = (f32[64]{0:T(128)S(1)}, f32[64,2048]{1,0:T(8,128)S(1)}) fusion(bf16[2048,2048]{1,0:T(8,128)(2,1)} %param.17, f32[64,2048]{1,0:T(8,128)S(1)} %multiply_reduce_fusion, f32[8,8,16,128]{3,2,1,0:T(8,128)S(1)} %bitcast.115, bf16[64,2048]{1,0:T(8,128)(2,1)S(1)} %copy-done.1), kind=kOutput, calls=%fused_computation.40 | convolution fusion | flops 537919424 | bytes 10223872 | tf_op jit(solution)/shard_map/dot_general | solution.py:115
  163.3 1.9 convolution_convert_fusion
  165.3 2.4 reshape.267
  167.7 0.4 pad_maximum_fusion
  168.1 98.4 %all_to_all.28 = bf16[32,28,2048]{2,1,0:T(8,128)(2,1)S(1)} all-to-all(bf16[32,28,2048]{2,1,0:T(8,128)(2,1)S(1)} %pad_maximum_fusion), channel_id=1, replica_groups=mesh['req'=4,'exp'=8] {'req','exp'}, dimensions={0} | all-to-all | bytes 7340032 | tf_op jit(solution)/shard_map/all_to_all | solution.py:140
  266.5 2.0 copy.96
  268.5 1.8 copy-done
  270.3 9.3 %fusion.2 = f32[4,32,7,704]{3,1,2,0:T(8,128)} fusion(bf16[32,4,7,2048]{3,0,2,1:T(8,128)(2,1)S(1)} %bitcast.116, bf16[4,2048,704]{1,2,0:T(8,128)(2,1)} %param.22), kind=kOutput, calls=%fused_computation.2 | convolution fusion | flops 2583691264 | bytes 17727488 | tf_op jit(solution)/shard_map/srcd,rdf->srcf/dot_general | solution.py:143
  279.7 14.0 %fusion.12 = bf16[4,32,7,2048]{3,1,2,0:T(8,128)(2,1)} fusion(bf16[4,704,2048]{2,1,0:T(8,128)(2,1)} %param.23, f32[4,32,7,704]{3,1,2,0:T(8,128)} %fusion.2, bf16[32,4,7,2048]{3,0,2,1:T(8,128)(2,1)} %bitcast.117, bf16[4,2048,704]{1,2,0:T(8,128)(2,1)} %param.21), kind=kOutput, calls=%fused_computation.15 | convolution fusion | flops 5173002240 | bytes 32931840 | tf_op jit(solution)/shard_map/srcf,rfd->srcd/dot_general | solution.py:145
  293.7 4.1 copy.97
  297.8 97.4 %all_to_all.29 = bf16[32,28,2048]{2,1,0:T(8,128)(2,1)} all-to-all(bf16[32,28,2048]{2,1,0:T(8,128)(2,1)S(1)} %copy.97), channel_id=1, replica_groups=mesh['req'=4,'exp'=8] {'req','exp'}, dimensions={0} | all-to-all | bytes 7340032 | tf_op jit(solution)/shard_map/all_to_all | solution.py:147
  395.2 5.8 %reshape.270 = bf16[2,448,2048]{2,1,0:T(8,128)(2,1)} reshape(bf16[32,28,2048]{2,1,0:T(8,128)(2,1)} %all_to_all.29) | data formatting | bytes 7340032 | tf_op jit(solution)/shard_map/reshape | solution.py:148
  401.0 3.0 reduce_sum.89
  404.1 1.1 fusion.19
  (30 shorter events, 0.6 us)
Async XLA Ops:
  6.5 55.0 %all-gather.2.cloned.1.call-start = ((), (), s32[]{:S(2)}) async-start(), calls=%async_computation.5 | async-start | bytes 2359296 | tf_op jit(solution)/shard_map/all_gather | solution.py:69
  71.1 10.7 %all-to-all-start = ((bf16[8,2,512]{2,1,0:T(2,128)(2,1)}), bf16[8,2,512]{2,1,0:T(2,128)(2,1)S(1)}, u32[]{:S(2)}, u32[]{:S(2)}) async-start(bf16[8,2,512]{2,1,0:T(2,128)(2,1)} %reshape.277), calls=%async_computation | async-start | bytes 32768 | tf_op jit(solution)/shard_map/all_to_all | solution.py:89
  81.7 20.4 %all-to-all-start.2 = ((bf16[8,2,512]{2,1,0:T(2,128)(2,1)}), bf16[8,2,512]{2,1,0:T(2,128)(2,1)S(1)}, u32[]{:S(2)}, u32[]{:S(2)}) async-start(bf16[8,2,512]{2,1,0:T(2,128)(2,1)} %reshape.279), calls=%async_computation.2 | async-start | bytes 32768 | tf_op jit(solution)/shard_map/all_to_all | solution.py:96
  99.3 8.9 %copy-start.2 = (s32[64,6]{0,1:T(8,128)S(1)}, s32[64,6]{0,1:T(8,128)}, u32[]{:S(2)}) copy-start(s32[64,6]{0,1:T(8,128)} %param.19) | copy-start | bytes 4612
  99.3 9.3 %copy-start.4 = (bf16[64,6]{0,1:T(8,128)(2,1)S(1)}, bf16[64,6]{0,1:T(8,128)(2,1)}, u32[]{:S(2)}) copy-start(bf16[64,6]{0,1:T(8,128)(2,1)} %param.20) | copy-start | bytes 2308
  102.2 52.9 %all-to-all-start.1 = ((bf16[8,64,2048]{2,1,0:T(8,128)(2,1)}), bf16[8,64,2048]{2,1,0:T(8,128)(2,1)S(1)}, u32[]{:S(2)}, u32[]{:S(2)}) async-start(bf16[8,64,2048]{2,1,0:T(8,128)(2,1)} %convert_element_type.97), calls=%async_computation.1 | async-start | bytes 4194304 | tf_op jit(solution)/shard_map/all_to_all | solution.py:103
  118.3 39.8 %copy-start.1 = (bf16[64,2048]{1,0:T(8,128)(2,1)S(1)}, bf16[64,2048]{1,0:T(8,128)(2,1)}, u32[]{:S(2)}) copy-start(bf16[64,2048]{1,0:T(8,128)(2,1)} %param.16) | copy-start | bytes 786436
  158.1 5.2 %copy-start.3 = (f32[2048]{0:T(1024)S(1)}, f32[2048]{0:T(1024)}, u32[]{:S(2)}) copy-start(f32[2048]{0:T(1024)} %param.18) | copy-start | bytes 24580
  268.5 1.8 copy-start
Sparse Core Ops, SparseCore 0:
  9.5 51.9 all-gather.1
where the time goes:
time: 413 us; the launch traced here: 412 us
  blocking collectives  196 us (47%)
  waiting for transfers between devices  88.2 us (21%)
  matrix products  45.7 us (11%)
  local copies, waits for them, and re-layouts  37.1 us (9%)
  other arithmetic  16.2 us (4%)
  starting transfers between devices  15.3 us (4%)
  between operations  13.7 us (3%)
    all_to_all x1, blocking collectives, shards(): lax.all_to_all(spread, ('req', 'exp'), split_axis=0, concat_axis=0, tiled...  98.4 us
    all_to_all x1, blocking collectives, shards(): lax.all_to_all(partial_out, ('req', 'exp'), split_axis=0, concat_axis=0,...  97.4 us
    all_gather x1, waiting for transfers between devices, shards(): q_all = lax.all_gather(query, 'exp', axis=0, tiled=True)  50.7 us
    all_to_all x1, waiting for transfers between devices, shards(): lax.all_to_all(partial_value.astype(jnp.bfloat16), 'exp', split_axis=0, c...  36.7 us
    dot_general x1, matrix products, shards(): jnp.einsum('srcf,rfd->srcd', hidden, w_down, preferred_element_type=jnp.f...  14 us
    dot_general x1, matrix products, shards(): jnp.einsum('srcd,rdf->srcf', pieces, w_up, preferred_element_type=jnp.flo...  9.33 us
  transfers between devices with their start and end apart: 4, of which 2 were waited for; matrix products, arithmetic and copies ran while one was open for 9% of the time, Pallas kernels for 0%

commit v1 on v0

--- a/solution.py
+++ b/solution.py
@@ -3,6 +3,8 @@
 import jax
 import jax.numpy as jnp
 from jax import lax
+from jax.experimental import pallas as pl
+from jax.experimental.pallas import tpu as pltpu
 from jax.sharding import PartitionSpec as P
 
 D = 2048
@@ -49,6 +51,307 @@
 def weighted_values(weights, values):
     vh = values.reshape(values.shape[0], KVH, HD)
     return jnp.einsum("qgjk,kgd->qgjd", weights, vh, preferred_element_type=jnp.float32)
+
+
+MESH = pl.DeviceIdType.MESH
+VMEM_SPEC = pl.BlockSpec(memory_space=pltpu.VMEM)
+ANY_SPEC = pl.BlockSpec(memory_space=pl.ANY)
+OFFSETS = (1, 3, 2)
+
+
+def place_here():
+    row, col = lax.axis_index("req"), lax.axis_index("exp")
+    return row // 2, col % 2, col // 2, row % 2
+
+
+def peer(x, y, z, c):
+    return (2 * x + c, 2 * z + y)
+
+
+def block_of(x, y, z, c):
+    return (2 * x + c) * 8 + 2 * z + y
+
+
+def stepped(x, y, c, da, db):
+    dx = jnp.where(c == 0, db, da)
+    dy = jnp.where(c == 0, da, db)
+    return jnp.bitwise_xor(x, dx), jnp.bitwise_xor(y, dy)
+
+
+def greet(peers):
+    barrier = pltpu.get_barrier_semaphore()
+    for other in peers:
+        pl.semaphore_signal(barrier, inc=1, device_id=other, device_id_type=MESH)
+    pl.semaphore_wait(barrier, len(peers))
+
+
+def partners(x, y, z, c):
+    xa, ya = stepped(x, y, c, 1, 0)
+    xb, yb = stepped(x, y, c, 0, 1)
+    along = {k: peer(x, y, (z + k) % 4, c) for k in OFFSETS}
+    return along, peer(xa, ya, z, c), peer(xb, yb, z, c), peer(x, y, z, 1 - c)
+
+
+def label(da, db, k):
+    return (da * 2 + db) * 4 + k
+
+
+def gather_kernel(mine_ref, out_ref, local_sem, send_sem, recv_sem):
+    x, y, z, c = place_here()
+    along, a_peer, b_peer, core_peer = partners(x, y, z, c)
+    greet([*along.values(), a_peer, b_peer, core_peer])
+    sent = []
+
+    def send(src, block, slot, target):
+        copy = pltpu.make_async_remote_copy(
+            src_ref=src,
+            dst_ref=out_ref.at[block],
+            send_sem=send_sem.at[len(sent)],
+            recv_sem=recv_sem.at[slot],
+            device_id=target,
+            device_id_type=MESH,
+        )
+        copy.start()
+        sent.append(copy)
+
+    def arrived(block, slot):
+        pltpu.make_async_remote_copy(
+            src_ref=mine_ref,
+            dst_ref=out_ref.at[block],
+            send_sem=send_sem.at[0],
+            recv_sem=recv_sem.at[slot],
+            device_id=core_peer,
+            device_id_type=MESH,
+        ).wait_recv()
+
+    def block(da, db, k):
+        xs, ys = stepped(x, y, c, da, db)
+        return block_of(xs, ys, (z + k) % 4, c)
+
+    own = block_of(x, y, z, c)
+    send(mine_ref, own, label(0, 1, 0), b_peer)
+    send(mine_ref, own, label(1, 0, 0), a_peer)
+    for k in OFFSETS:
+        send(mine_ref, own, label(0, 0, (4 - k) % 4), along[k])
+    send(mine_ref, own, 16 + label(0, 0, 0), core_peer)
+    keep = pltpu.make_async_copy(mine_ref, out_ref.at[own], local_sem)
+    keep.start()
+
+    def relay(da, db, k):
+        b = block(da, db, k)
+        arrived(b, label(da, db, k))
+        if db == 0:
+            send(out_ref.at[b], b, label(da, 1, k), b_peer)
+            if da == 0:
+                send(out_ref.at[b], b, label(1, 0, k), a_peer)
+        send(out_ref.at[b], b, 16 + label(da, db, k), core_peer)
+
+    relay(1, 0, 0)
+    for k in OFFSETS:
+        relay(0, 0, k)
+    relay(0, 1, 0)
+    for k in OFFSETS:
+        relay(1, 0, k)
+    relay(1, 1, 0)
+    for k in OFFSETS:
+        relay(0, 1, k)
+    for k in OFFSETS:
+        relay(1, 1, k)
+    for da in range(2):
+        for db in range(2):
+            for k in range(4):
+                xs, ys = stepped(x, y, 1 - c, da, db)
+                arrived(block_of(xs, ys, (z + k) % 4, 1 - c), 16 + label(da, db, k))
+    keep.wait()
+    for copy in sent:
+        copy.wait_send()
+
+
+def gather_rows(mine):
+    rows, width = mine.shape
+    return pl.pallas_call(
+        gather_kernel,
+        out_shape=jax.ShapeDtypeStruct((32, rows, width), mine.dtype),
+        in_specs=[VMEM_SPEC],
+        out_specs=ANY_SPEC,
+        scratch_shapes=[
+            pltpu.SemaphoreType.DMA(()),
+            pltpu.SemaphoreType.DMA((31,)),
+            pltpu.SemaphoreType.DMA((32,)),
+        ],
+        compiler_params=pltpu.CompilerParams(collective_id=1, has_side_effects=True),
+        name="gather_rows",
+    )(mine)
+
+
+def reduce_kernel(
+    part_ref, stream_ref, out_ref, in_c, in_b, in_a, in_z, sum_c, sum_b, sum_a, send_sem, recv_sem
+):
+    x, y, z, c = place_here()
+    along, a_peer, b_peer, core_peer = partners(x, y, z, c)
+    greet([*along.values(), a_peer, b_peer, core_peer])
+    sent = []
+    f32 = jnp.float32
+
+    def send(src, dst, slot, target):
+        copy = pltpu.make_async_remote_copy(
+            src_ref=src,
+            dst_ref=dst,
+            send_sem=send_sem.at[len(sent)],
+            recv_sem=recv_sem.at[slot],
+            device_id=target,
+            device_id_type=MESH,
+        )
+        copy.start()
+        sent.append(copy)
+
+    def arrived(dst, slot):
+        pltpu.make_async_remote_copy(
+            src_ref=dst,
+            dst_ref=dst,
+            send_sem=send_sem.at[0],
+            recv_sem=recv_sem.at[slot],
+            device_id=core_peer,
+            device_id_type=MESH,
+        ).wait_recv()
+
+    def add(dst, one, two):
+        rows = dst.shape[0]
+
+        @pl.loop(0, rows // 16)
+        def _(i):
+            part = pl.ds(pl.multiple_of(i * 16, 16), 16)
+            dst[part, :] = (one[part, :].astype(f32) + two[part, :].astype(f32)).astype(dst.dtype)
+
+    ks = (*OFFSETS, 0)
+    order = [(da, db, k) for db in (1, 0) for da in (1, 0) for k in ks]
+    for da, db, k in order:
+        xs, ys = stepped(x, y, 1 - c, da, db)
+        i = label(da, db, k)
+        send(part_ref.at[block_of(xs, ys, (z + k) % 4, 1 - c)], in_c.at[i], i, core_peer)
+    for da, db, k in order:
+        i = label(da, db, k)
+        xs, ys = stepped(x, y, c, da, db)
+        arrived(in_c.at[i], i)
+        add(sum_c.at[i], part_ref.at[block_of(xs, ys, (z + k) % 4, c)], in_c.at[i])
+        if db == 1:
+            send(sum_c.at[i], in_b.at[da * 4 + k], 16 + da * 4 + k, b_peer)
+    for da in (1, 0):
+        for k in ks:
+            j = da * 4 + k
+            arrived(in_b.at[j], 16 + j)
+            add(sum_b.at[j], sum_c.at[label(da, 0, k)], in_b.at[j])
+            if da == 1:
+                send(sum_b.at[j], in_a.at[k], 24 + k, a_peer)
+    for k in ks:
+        arrived(in_a.at[k], 24 + k)
+        add(sum_a.at[k], sum_b.at[k], in_a.at[k])
+        if k:
+            send(sum_a.at[k], in_z.at[4 - k], 28 + (4 - k), along[k])
+    for k in OFFSETS:
+        arrived(in_z.at[k], 28 + k)
+    rows = out_ref.shape[0]
+
+    @pl.loop(0, rows // 16)
+    def _(i):
+        part = pl.ds(pl.multiple_of(i * 16, 16), 16)
+        whole = sum_a[0, part, :].astype(f32)
+        for k in OFFSETS:
+            whole += in_z[k, part, :].astype(f32)
+        out_ref[part, :] = (stream_ref[part, :].astype(f32) + whole).astype(out_ref.dtype)
+
+    for copy in sent:
+        copy.wait_send()
+
+
+def reduce_rows(part, stream):
+    rows, width = stream.shape
+    space = lambda n: pltpu.VMEM((n, rows, width), jnp.bfloat16)
+    return pl.pallas_call(
+        reduce_kernel,
+        out_shape=jax.ShapeDtypeStruct(stream.shape, stream.dtype),
+        in_specs=[VMEM_SPEC, VMEM_SPEC],
+        out_specs=VMEM_SPEC,
+        scratch_shapes=[
+            space(16),
+            space(8),
+            space(4),
+            space(4),
+            space(16),
+            space(8),
+            space(4),
+            pltpu.SemaphoreType.DMA((31,)),
+            pltpu.SemaphoreType.DMA((32,)),
+        ],
+        compiler_params=pltpu.CompilerParams(
+            collective_id=2, has_side_effects=True, vmem_limit_bytes=48 * 2**20
+        ),
+        name="reduce_rows",
+    )(part, stream)
+
+
+def expert_kernel(rows_ref, gate_ref, up_ref, down_ref, out_ref):
+    groups, _, count, width = rows_ref.shape
+    rows = rows_ref[...].reshape(groups * count, width)
+    gate = jnp.dot(rows, gate_ref[0], preferred_element_type=jnp.float32)
+    up = jnp.dot(rows, up_ref[0], preferred_element_type=jnp.float32)
+    hidden = (gate / (1.0 + jnp.exp(-gate)) * up).astype(jnp.bfloat16)
+    part = jnp.dot(hidden, down_ref[0], preferred_element_type=jnp.float32)
+    out_ref[...] = part.astype(jnp.bfloat16).reshape(groups, 1, count, width)
+
+
+def run_experts(rows, w_gate, w_up, w_down):
+    groups, here, count, width = rows.shape
+    ff = w_gate.shape[2]
+    lot = pl.BlockSpec((groups, 1, count, width), lambda r: (0, r, 0, 0))
+    return pl.pallas_call(
+        expert_kernel,
+        out_shape=jax.ShapeDtypeStruct(rows.shape, rows.dtype),
+        grid=(here,),
+        in_specs=[
+            lot,
+            pl.BlockSpec((1, width, ff), lambda r: (r, 0, 0)),
+            pl.BlockSpec((1, width, ff), lambda r: (r, 0, 0)),
+            pl.BlockSpec((1, ff, width), lambda r: (r, 0, 0)),
+        ],
+        out_specs=lot,
+        compiler_params=pltpu.CompilerParams(vmem_limit_bytes=48 * 2**20),
+        name="run_experts",
+    )(rows, w_gate, w_up, w_down)
+
+
+def routed(stream, normed, routes, gates, w_gate, w_up, w_down):
+    tok_rows = stream.shape[0]
+    rows_here = w_gate.shape[0]
+    axes = ("req", "exp")
+    me = lax.axis_index("req") * lax.axis_size("exp") + lax.axis_index("exp")
+    flat = routes.reshape(-1)
+    hits = (flat[:, None] == jnp.arange(EXPERTS, dtype=jnp.int32)[None, :]).astype(jnp.int32)
+    slot = jnp.sum(hits * (jnp.cumsum(hits, axis=0) - 1), axis=1)
+    place = (flat * CAP + slot).reshape(tok_rows, TOPK)
+    places = lax.all_gather(place, axes, axis=0, tiled=True)
+    shares = lax.all_gather(gates, axes, axis=0, tiled=True).astype(jnp.float32)
+    tokens = places.shape[0]
+    first = me * rows_here % EXPERTS * CAP
+    rel = places - first
+    lot = jnp.arange(tokens, dtype=jnp.int32)[:, None] // tok_rows % 4
+    row = rel // CAP * 32 + lot * CAP + rel % CAP
+    row = jnp.where((rel >= 0) & (rel < rows_here * CAP), row, -1).reshape(8, tokens // 8, TOPK)
+    shares = shares.reshape(8, tokens // 8, TOPK)
+    lanes = jnp.arange(rows_here * 32, dtype=jnp.int32)
+    pick = jnp.zeros((8, tokens // 8, rows_here * 32), jnp.float32)
+    mixer = pick
+    for k in range(TOPK):
+        same = row[:, :, k : k + 1] == lanes
+        pick = jnp.where(same, 1.0, pick)
+        mixer = jnp.where(same, shares[:, :, k : k + 1], mixer)
+    pick, mixer = pick.astype(jnp.bfloat16), mixer.astype(jnp.bfloat16)
+    everyone = gather_rows(normed).reshape(8, tokens // 8, D)
+    rows = jnp.einsum("gtp,gtd->gpd", pick, everyone, preferred_element_type=jnp.float32)
+    rows = rows.astype(jnp.bfloat16).reshape(8, rows_here, 32, D)
+    outs = run_experts(rows, w_gate, w_up, w_down).reshape(8, rows_here * 32, D)
+    part = jnp.einsum("gtp,gpd->gtd", mixer, outs, preferred_element_type=jnp.float32)
+    return reduce_rows(part.astype(jnp.bfloat16).reshape(-1, tok_rows, D), stream)
 
 
 def shards(
@@ -120,6 +423,8 @@
     ).astype(jnp.bfloat16)
     rows_here = w_gate.shape[0]
     devices = n_req * n_exp
+    if (n_req, n_exp, tok_rows) == (4, 8, 64):
+        return routed(stream, normed, routes, gates, w_gate, w_up, w_down)
     flat = routes.reshape(-1)
     hits = (flat[:, None] == jnp.arange(EXPERTS, dtype=jnp.int32)[None, :]).astype(jnp.int32)
     slot = jnp.sum(hits * (jnp.cumsum(hits, axis=0) - 1), axis=1)

time: 413 us -> 479 us (1.16)
  Pallas kernels: 0 us -> 130 us
  blocking collectives: 196 us -> 164 us
  waiting for transfers between devices: 88.2 us -> 57.1 us
  local copies, waits for them, and re-layouts: 37.1 us -> 58.8 us
  matrix products: 45.7 us -> 31 us
  other arithmetic: 16.2 us -> 9.65 us
    all_to_all x2 -> x0, blocking collectives: 196 us -> none  [the longest x1 98.4 us: shards(): lax.all_to_all(spread, ('req', 'exp'), split_axis=0, concat_axis=0, tiled...]
    all_gather x0 -> x2, blocking collectives: none -> 164 us  [the longest x1 100 us: routed(): places = lax.all_gather(place, axes, axis=0, tiled=True)]
    pallas_call x0 -> x3, Pallas kernels: none -> 130 us  [the longest x1 70.2 us: reduce_rows(): pl.pallas_call(reduce_kernel, out_shape=jax.ShapeDtypeStruct(stream.shape...]
    all_to_all x1, waiting for transfers between devices: 36.7 us -> 0.01 us  [shards(): lax.all_to_all(partial_value.astype(jnp.bfloat16), 'exp', split_axis=0, c...]
    unnamed x15 -> x19, local copies, waits for them, and re-layouts: 3.49 us -> 39 us
    reshape x3 -> x1, local copies, waits for them, and re-layouts: 12.3 us -> 0.11 us  [routed(): shares = shares.reshape(8, tokens // 8, TOPK)]
    dot_general x4 -> x2, matrix products: 26.5 us -> 15.7 us  [the longest x1 8.17 us: routed(): jnp.einsum('gtp,gpd->gtd', mixer, outs, preferred_element_type=jnp.float32)]
    all_to_all x1, waiting for transfers between devices: 0.01 us -> 5.6 us  [shards(): lax.all_to_all(total.reshape(count, H).astype(jnp.bfloat16), 'exp', split...]
  transfers between devices with their start and end apart: 4 -> 4, of which waited for: 2 -> 2; matrix products, arithmetic and copies ran while one was open for 9% -> 13% of each run, Pallas kernels for 0% -> 0%
where the time goes in v1:
time: 479 us; the launch traced here: 477 us
  blocking collectives  164 us (34%)
  Pallas kernels  130 us (27%)
  local copies, waits for them, and re-layouts  58.8 us (12%)
  waiting for transfers between devices  57.1 us (12%)
  matrix products  31 us (6%)
  between operations  13.7 us (3%)
  starting transfers between devices  12.6 us (3%)
  other arithmetic  9.65 us (2%)
    all_gather x1, blocking collectives, routed(): places = lax.all_gather(place, axes, axis=0, tiled=True)  100 us
    pallas_call x1, Pallas kernels, reduce_rows(): pl.pallas_call(reduce_kernel, out_shape=jax.ShapeDtypeStruct(stream.shape...  70.2 us
    all_gather x1, blocking collectives, routed(): shares = lax.all_gather(gates, axes, axis=0, tiled=True).astype(jnp.float32)  63.8 us
    all_gather x1, waiting for transfers between devices, shards(): q_all = lax.all_gather(query, 'exp', axis=0, tiled=True)  50.8 us
    pallas_call x1, Pallas kernels, gather_rows(): pl.pallas_call(gather_kernel, out_shape=jax.ShapeDtypeStruct((32, rows, w...  43.4 us
    unnamed x19, local copies, waits for them, and re-layouts  39 us
    pallas_call x1, Pallas kernels, run_experts(): pl.pallas_call(expert_kernel, out_shape=jax.ShapeDtypeStruct(rows.shape,...  16.4 us
  transfers between devices with their start and end apart: 4, of which 2 were waited for; matrix products, arithmetic and copies ran while one was open for 13% of the time, Pallas kernels for 0%

profile of v1, /device:TPU:0, one launch (start us, length us, event | category | flops | bytes accessed | tf_op | source)
XLA Modules:
  0.0 477.1 jit_solution(8294790319326756601)
XLA Ops:
  6.5 0.7 all-gather.4.cloned.1.call-update
  7.3 1.2 pad_maximum_fusion
  8.5 1.2 dynamic_slice.3
  9.7 0.7 fusion.61
  10.4 0.3 select_and_fusion
  10.7 50.8 %all-gather.4.cloned.1.call-done = bf16[512,2048]{1,0:T(8,128)(2,1)} async-done(((bf16[64,2048]{1,0:T(8,128)(2,1)}), bf16[512,2048]{1,0:T(8,128)(2,1)}) %all-gather.4.cloned.1.call-update) | async-done | bytes 2097168 | tf_op jit(solution)/shard_map/all_gather | solution.py:372
  61.5 2.9 copy.87
  64.4 1.9 fusion
  66.3 4.0 copy-done
  70.3 2.6 fusion.1
  72.9 0.1 convert_element_type.86
  73.0 0.7 reshape.352
  73.7 3.3 all-to-all-start.2
  77.3 0.7 reshape.350
  78.0 5.6 %all-to-all-done.2 = bf16[8,2,512]{2,1,0:T(2,128)(2,1)S(1)} async-done(((bf16[8,2,512]{2,1,0:T(2,128)(2,1)}), bf16[8,2,512]{2,1,0:T(2,128)(2,1)S(1)}, u32[]{:S(2)}, u32[]{:S(2)}) %all-to-all-start.2) | async-done | bytes 16416 | tf_op jit(solution)/shard_map/all_to_all | solution.py:399
  83.6 3.3 all-to-all-start
  86.9 8.2 %convert_bitcast_fusion = bf16[512,4,4,128]{0,3,2,1:T(8,128)(2,1)} fusion(f32[4,320,512,4]{2,1,3,0:T(8,128)} %copy-done, f32[512,4,4]{0,2,1:T(4,128)S(1)} %get-tuple-element.25, pred[512,320]{0,1:T(8,128)(4,1)S(1)} %select_and_fusion, bf16[320,4,128,1]{2,1,0,3:T(4,128)(2,1)S(1)} %bitcast.120), kind=kOutput, calls=%fused_computation.12 | convolution fusion | flops 685244416 | bytes 13107200 | tf_op jit(solution)/shard_map/qgjk,kgd->qgjd/dot_general | solution.py:53
  95.1 3.4 copy.93
  98.5 2.8 convert_element_type.83
  101.3 5.9 %all-to-all-start.1 = ((bf16[8,64,2048]{2,1,0:T(8,128)(2,1)}), bf16[8,64,2048]{2,1,0:T(8,128)(2,1)S(1)}, u32[]{:S(2)}, u32[]{:S(2)}) async-start(bf16[8,64,2048]{2,1,0:T(8,128)(2,1)} %convert_element_type.83), calls=%async_computation.1 | async-start | bytes 4194304 | tf_op jit(solution)/shard_map/all_to_all | solution.py:406
  107.3 0.1 copy.81
  107.4 0.1 eq.158
  107.5 0.1 eq.154
  107.7 0.9 reduce-window.6
  108.6 0.2 slice_reduce_fusion
  108.8 0.1 fusion.40
  109.0 0.1 reduce_sum.52
  109.2 100.4 %all-gather = s32[32,64,6]{1,2,0:T(8,128)S(1)} all-gather(s32[1,64,6]{1,2,0:T(8,128)S(1)} %add_bitcast_fusion.1), channel_id=1, replica_groups=mesh['req'=4,'exp'=8] {'req','exp'}, dimensions={0}, use_global_device_ids=true | all-gather | bytes 50688 | tf_op jit(solution)/shard_map/all_gather | solution.py:332
  209.9 0.1 reshape.343
  210.0 0.1 reshape.345
  210.3 16.3 %copy.98.gate_ref = bf16[4,2048,704]{2,1,0:T(8,128)(2,1)} copy(bf16[4,2048,704]{1,2,0:T(8,128)(2,1)} %param.21) | data formatting | bytes 23068672 | tf_op args[9]
  226.6 16.3 %copy.99.up_ref = bf16[4,2048,704]{2,1,0:T(8,128)(2,1)} copy(bf16[4,2048,704]{1,2,0:T(8,128)(2,1)} %param.22) | data formatting | bytes 23068672 | tf_op args[10]
  242.8 63.8 %all-gather.1 = bf16[32,64,6]{1,2,0:T(8,128)(2,1)S(1)} all-gather(bf16[1,64,6]{1,2,0:T(8,128)(2,1)S(1)} %bitcast.126), channel_id=1, replica_groups=mesh['req'=4,'exp'=8] {'req','exp'}, dimensions={0}, use_global_device_ids=true | all-gather | bytes 25344 | tf_op jit(solution)/shard_map/all_gather | solution.py:333
  306.7 0.1 reshape.324
  306.8 0.1 reshape.351
  307.1 0.1 copy.91
  307.2 2.6 mul.99
  309.8 4.9 %mul.100 = f32[8,64,2048]{2,1,0:T(8,128)} reshape(f32[8,64,16,128]{3,2,1,0:T(8,128)} %mul.99) | data formatting | bytes 8388608 | tf_op jit(solution)/shard_map/mul | solution.py:415
  314.8 2.8 multiply_reduce_fusion
  317.6 0.2 div.70
  317.8 5.2 %fusion.9 = (f32[64]{0:T(128)S(1)}, bf16[64,2048]{1,0:T(8,128)(2,1)S(1)}) fusion(bf16[2048,2048]{1,0:T(8,128)(2,1)} %param.17, f32[64,2048]{1,0:T(8,128)S(1)} %multiply_reduce_fusion, f32[8,8,16,128]{3,2,1,0:T(8,128)S(1)} %bitcast.117, bf16[64,2048]{1,0:T(8,128)(2,1)S(1)} %copy-done.1), kind=kOutput, calls=%fused_computation.26 | convolution fusion | flops 537919424 | bytes 9961728 | tf_op jit(solution)/shard_map/dot_general | solution.py:418
  323.0 0.8 fusion.11.mine_ref
  323.9 43.4 %gather_rows.1 = bf16[32,64,2048]{2,1,0:T(8,128)(2,1)} custom-call(bf16[64,2048]{1,0:T(8,128)(2,1)} %fusion.11.mine_ref), custom_call_target="tpu_custom_call" | custom-call | tf_op jit(solution)/shard_map/gather_rows/pallas_call | solution.py:172
  367.3 7.5 %convolution_convert_fusion.1 = bf16[8,128,2048]{2,1,0:T(8,128)(2,1)} fusion(bf16[8,256,2048]{2,1,0:T(8,128)(2,1)} %bitcast.113, s32[8,256]{1,0:T(8,128)S(1)} %get-tuple-element.12, s32[8,256]{1,0:T(8,128)S(1)} %get-tuple-element.13, s32[8,256]{1,0:T(8,128)S(1)} %get-tuple-element.14, s32[8,256]{1,0:T(8,128)S(1)} %get-tuple-element.15, ...), kind=kOutput, calls=%fused_computation.9 | convolution fusion | flops 1079246848 | bytes 12632064 | tf_op jit(solution)/shard_map/gtp,gtd->gpd/dot_general | solution.py:350
  374.8 16.4 %run_experts.1 = bf16[8,4,32,2048]{3,2,1,0:T(8,128)(2,1)S(1)} custom-call(bf16[8,4,32,2048]{3,2,1,0:T(8,128)(2,1)} %bitcast.115, bf16[4,2048,704]{2,1,0:T(8,128)(2,1)} %copy.98.gate_ref, bf16[4,2048,704]{2,1,0:T(8,128)(2,1)} %copy.99.up_ref, bf16[4,704,2048]{2,1,0:T(8,128)(2,1)} %down_ref.1), custom_call_target="tpu_custom_call" | custom-call | tf_op jit(solution)/shard_map/run_experts/pallas_call | solution.py:307
  391.2 8.2 %convolution_convert_fusion = bf16[8,256,2048]{2,1,0:T(8,128)(2,1)} fusion(bf16[8,128,2048]{2,1,0:T(8,128)(2,1)S(1)} %bitcast.112, bf16[8,256]{1,0:T(8,128)(2,1)S(1)} %get-tuple-element.20, s32[8,256]{1,0:T(8,128)S(1)} %get-tuple-element.12, bf16[8,256]{1,0:T(8,128)(2,1)S(1)} %get-tuple-element.21, s32[8,256]{1,0:T(8,128)S(1)} %get-tuple-element.13, ...), kind=kOutput, calls=%fused_computation.5 | convolution fusion | flops 1081081856 | bytes 12656640 | tf_op jit(solution)/shard_map/gtp,gpd->gtd/dot_general | solution.py:353
  399.4 70.2 %reduce_rows.1 = bf16[64,2048]{1,0:T(8,128)(2,1)S(1)} custom-call(bf16[32,64,2048]{2,1,0:T(8,128)(2,1)} %bitcast.114, bf16[64,2048]{1,0:T(8,128)(2,1)S(1)} %get-tuple-element.28.stream_ref), custom_call_target="tpu_custom_call" | custom-call | tf_op jit(solution)/shard_map/reduce_rows/pallas_call | solution.py:270
  469.6 0.7 copy.141
  (40 shorter events, 1.1 us)
Async XLA Ops:
  6.5 55.0 %all-gather.4.cloned.1.call-start = ((), (), s32[]{:S(2)}) async-start(), calls=%async_computation.3 | async-start | bytes 2359296 | tf_op jit(solution)/shard_map/all_gather | solution.py:372
  66.3 4.0 copy-start
  73.7 9.8 %all-to-all-start.2 = ((bf16[8,2,512]{2,1,0:T(2,128)(2,1)}), bf16[8,2,512]{2,1,0:T(2,128)(2,1)S(1)}, u32[]{:S(2)}, u32[]{:S(2)}) async-start(bf16[8,2,512]{2,1,0:T(2,128)(2,1)} %reshape.352), calls=%async_computation.2 | async-start | bytes 32768 | tf_op jit(solution)/shard_map/all_to_all | solution.py:399
  83.6 17.8 %all-to-all-start = ((bf16[8,2,512]{2,1,0:T(2,128)(2,1)}), bf16[8,2,512]{2,1,0:T(2,128)(2,1)S(1)}, u32[]{:S(2)}, u32[]{:S(2)}) async-start(bf16[8,2,512]{2,1,0:T(2,128)(2,1)} %reshape.350), calls=%async_computation | async-start | bytes 32768 | tf_op jit(solution)/shard_map/all_to_all | solution.py:392
  95.1 12.2 %copy-start.2 = (s32[64,6]{0,1:T(8,128)S(1)}, s32[64,6]{0,1:T(8,128)}, u32[]{:S(2)}) copy-start(s32[64,6]{0,1:T(8,128)} %param.19) | copy-start | bytes 4612
  101.3 213.5 %all-to-all-start.1 = ((bf16[8,64,2048]{2,1,0:T(8,128)(2,1)}), bf16[8,64,2048]{2,1,0:T(8,128)(2,1)S(1)}, u32[]{:S(2)}, u32[]{:S(2)}) async-start(bf16[8,64,2048]{2,1,0:T(8,128)(2,1)} %convert_element_type.83), calls=%async_computation.1 | async-start | bytes 4194304 | tf_op jit(solution)/shard_map/all_to_all | solution.py:406
  226.6 16.3 %copy-start.4 = (bf16[64,6]{0,1:T(8,128)(2,1)S(1)}, bf16[64,6]{0,1:T(8,128)(2,1)}, u32[]{:S(2)}) copy-start(bf16[64,6]{0,1:T(8,128)(2,1)} %param.20) | copy-start | bytes 2308
  309.8 8.0 %copy-start.1 = (bf16[64,2048]{1,0:T(8,128)(2,1)S(1)}, bf16[64,2048]{1,0:T(8,128)(2,1)}, u32[]{:S(2)}) copy-start(bf16[64,2048]{1,0:T(8,128)(2,1)} %param.16) | copy-start | bytes 786436
  317.8 5.2 %copy-start.3 = (f32[2048]{0:T(1024)S(1)}, f32[2048]{0:T(1024)}, u32[]{:S(2)}) copy-start(f32[2048]{0:T(1024)} %param.18) | copy-start | bytes 24580
Sparse Core Ops, SparseCore 0:
  9.5 51.9 all-gather.3

commit v2 on v1

--- a/solution.py
+++ b/solution.py
@@ -96,55 +96,59 @@
     return (da * 2 + db) * 4 + k
 
 
-def gather_kernel(mine_ref, out_ref, local_sem, send_sem, recv_sem):
+def gather_kernel(mine_ref, note_ref, out_ref, notes_ref, local_sem, send_sem, recv_sem):
     x, y, z, c = place_here()
     along, a_peer, b_peer, core_peer = partners(x, y, z, c)
     greet([*along.values(), a_peer, b_peer, core_peer])
     sent = []
 
-    def send(src, block, slot, target):
-        copy = pltpu.make_async_remote_copy(
-            src_ref=src,
-            dst_ref=out_ref.at[block],
-            send_sem=send_sem.at[len(sent)],
-            recv_sem=recv_sem.at[slot],
-            device_id=target,
-            device_id_type=MESH,
-        )
-        copy.start()
-        sent.append(copy)
+    def send(src, note, block, slot, target):
+        for lane, (one, dst) in enumerate(((note, notes_ref), (src, out_ref))):
+            copy = pltpu.make_async_remote_copy(
+                src_ref=one,
+                dst_ref=dst.at[block],
+                send_sem=send_sem.at[len(sent)],
+                recv_sem=recv_sem.at[2 * slot + lane],
+                device_id=target,
+                device_id_type=MESH,
+            )
+            copy.start()
+            sent.append(copy)
 
     def arrived(block, slot):
-        pltpu.make_async_remote_copy(
-            src_ref=mine_ref,
-            dst_ref=out_ref.at[block],
-            send_sem=send_sem.at[0],
-            recv_sem=recv_sem.at[slot],
-            device_id=core_peer,
-            device_id_type=MESH,
-        ).wait_recv()
+        for lane, (one, dst) in enumerate(((note_ref, notes_ref), (mine_ref, out_ref))):
+            pltpu.make_async_remote_copy(
+                src_ref=one,
+                dst_ref=dst.at[block],
+                send_sem=send_sem.at[0],
+                recv_sem=recv_sem.at[2 * slot + lane],
+                device_id=core_peer,
+                device_id_type=MESH,
+            ).wait_recv()
 
     def block(da, db, k):
         xs, ys = stepped(x, y, c, da, db)
         return block_of(xs, ys, (z + k) % 4, c)
 
     own = block_of(x, y, z, c)
-    send(mine_ref, own, label(0, 1, 0), b_peer)
-    send(mine_ref, own, label(1, 0, 0), a_peer)
-    for k in OFFSETS:
-        send(mine_ref, own, label(0, 0, (4 - k) % 4), along[k])
-    send(mine_ref, own, 16 + label(0, 0, 0), core_peer)
-    keep = pltpu.make_async_copy(mine_ref, out_ref.at[own], local_sem)
+    send(mine_ref, note_ref, own, label(0, 1, 0), b_peer)
+    send(mine_ref, note_ref, own, label(1, 0, 0), a_peer)
+    for k in OFFSETS:
+        send(mine_ref, note_ref, own, label(0, 0, (4 - k) % 4), along[k])
+    send(mine_ref, note_ref, own, 16 + label(0, 0, 0), core_peer)
+    keep = pltpu.make_async_copy(mine_ref, out_ref.at[own], local_sem.at[0])
     keep.start()
+    jot = pltpu.make_async_copy(note_ref, notes_ref.at[own], local_sem.at[1])
+    jot.start()
 
     def relay(da, db, k):
         b = block(da, db, k)
         arrived(b, label(da, db, k))
         if db == 0:
-            send(out_ref.at[b], b, label(da, 1, k), b_peer)
+            send(out_ref.at[b], notes_ref.at[b], b, label(da, 1, k), b_peer)
             if da == 0:
-                send(out_ref.at[b], b, label(1, 0, k), a_peer)
-        send(out_ref.at[b], b, 16 + label(da, db, k), core_peer)
+                send(out_ref.at[b], notes_ref.at[b], b, label(1, 0, k), a_peer)
+        send(out_ref.at[b], notes_ref.at[b], b, 16 + label(da, db, k), core_peer)
 
     relay(1, 0, 0)
     for k in OFFSETS:
@@ -163,25 +167,26 @@
                 xs, ys = stepped(x, y, 1 - c, da, db)
                 arrived(block_of(xs, ys, (z + k) % 4, 1 - c), 16 + label(da, db, k))
     keep.wait()
+    jot.wait()
     for copy in sent:
         copy.wait_send()
 
 
-def gather_rows(mine):
-    rows, width = mine.shape
+def gather_rows(mine, note):
+    whole = lambda one: jax.ShapeDtypeStruct((32, *one.shape), one.dtype)
     return pl.pallas_call(
         gather_kernel,
-        out_shape=jax.ShapeDtypeStruct((32, rows, width), mine.dtype),
-        in_specs=[VMEM_SPEC],
-        out_specs=ANY_SPEC,
+        out_shape=(whole(mine), whole(note)),
+        in_specs=[VMEM_SPEC, VMEM_SPEC],
+        out_specs=(ANY_SPEC, ANY_SPEC),
         scratch_shapes=[
-            pltpu.SemaphoreType.DMA(()),
-            pltpu.SemaphoreType.DMA((31,)),
-            pltpu.SemaphoreType.DMA((32,)),
+            pltpu.SemaphoreType.DMA((2,)),
+            pltpu.SemaphoreType.DMA((62,)),
+            pltpu.SemaphoreType.DMA((64,)),
         ],
         compiler_params=pltpu.CompilerParams(collective_id=1, has_side_effects=True),
         name="gather_rows",
-    )(mine)
+    )(mine, note)
 
 
 def reduce_kernel(
@@ -293,8 +298,9 @@
 def expert_kernel(rows_ref, gate_ref, up_ref, down_ref, out_ref):
     groups, _, count, width = rows_ref.shape
     rows = rows_ref[...].reshape(groups * count, width)
-    gate = jnp.dot(rows, gate_ref[0], preferred_element_type=jnp.float32)
-    up = jnp.dot(rows, up_ref[0], preferred_element_type=jnp.float32)
+    across = (((1,), (1,)), ((), ()))
+    gate = lax.dot_general(rows, gate_ref[0], across, preferred_element_type=jnp.float32)
+    up = lax.dot_general(rows, up_ref[0], across, preferred_element_type=jnp.float32)
     hidden = (gate / (1.0 + jnp.exp(-gate)) * up).astype(jnp.bfloat16)
     part = jnp.dot(hidden, down_ref[0], preferred_element_type=jnp.float32)
     out_ref[...] = part.astype(jnp.bfloat16).reshape(groups, 1, count, width)
@@ -310,28 +316,33 @@
         grid=(here,),
         in_specs=[
             lot,
-            pl.BlockSpec((1, width, ff), lambda r: (r, 0, 0)),
-            pl.BlockSpec((1, width, ff), lambda r: (r, 0, 0)),
+            pl.BlockSpec((1, ff, width), lambda r: (r, 0, 0)),
+            pl.BlockSpec((1, ff, width), lambda r: (r, 0, 0)),
             pl.BlockSpec((1, ff, width), lambda r: (r, 0, 0)),
         ],
         out_specs=lot,
         compiler_params=pltpu.CompilerParams(vmem_limit_bytes=48 * 2**20),
         name="run_experts",
-    )(rows, w_gate, w_up, w_down)
+    )(rows, w_gate.swapaxes(1, 2), w_up.swapaxes(1, 2), w_down)
 
 
 def routed(stream, normed, routes, gates, w_gate, w_up, w_down):
     tok_rows = stream.shape[0]
     rows_here = w_gate.shape[0]
-    axes = ("req", "exp")
     me = lax.axis_index("req") * lax.axis_size("exp") + lax.axis_index("exp")
     flat = routes.reshape(-1)
     hits = (flat[:, None] == jnp.arange(EXPERTS, dtype=jnp.int32)[None, :]).astype(jnp.int32)
     slot = jnp.sum(hits * (jnp.cumsum(hits, axis=0) - 1), axis=1)
-    place = (flat * CAP + slot).reshape(tok_rows, TOPK)
-    places = lax.all_gather(place, axes, axis=0, tiled=True)
-    shares = lax.all_gather(gates, axes, axis=0, tiled=True).astype(jnp.float32)
-    tokens = places.shape[0]
+    note = jnp.concatenate(
+        [routes.astype(gates.dtype), slot.reshape(tok_rows, TOPK).astype(gates.dtype), gates], 1
+    )
+    note = jnp.pad(note, ((0, 0), (0, 128 - 3 * TOPK)))
+    everyone, notes = gather_rows(normed, note)
+    tokens = everyone.shape[0] * tok_rows
+    everyone = everyone.reshape(8, tokens // 8, D)
+    notes = notes.reshape(tokens, 128).astype(jnp.float32)
+    places = (notes[:, :TOPK] * CAP + notes[:, TOPK : 2 * TOPK]).astype(jnp.int32)
+    shares = notes[:, 2 * TOPK : 3 * TOPK]
     first = me * rows_here % EXPERTS * CAP
     rel = places - first
     lot = jnp.arange(tokens, dtype=jnp.int32)[:, None] // tok_rows % 4
@@ -346,7 +357,6 @@
         pick = jnp.where(same, 1.0, pick)
         mixer = jnp.where(same, shares[:, :, k : k + 1], mixer)
     pick, mixer = pick.astype(jnp.bfloat16), mixer.astype(jnp.bfloat16)
-    everyone = gather_rows(normed).reshape(8, tokens // 8, D)
     rows = jnp.einsum("gtp,gtd->gpd", pick, everyone, preferred_element_type=jnp.float32)
     rows = rows.astype(jnp.bfloat16).reshape(8, rows_here, 32, D)
     outs = run_experts(rows, w_gate, w_up, w_down).reshape(8, rows_here * 32, D)

time: 479 us -> 343 us (0.72)
  blocking collectives: 164 us -> 0 us
  waiting for transfers between devices: 57.1 us -> 87.5 us
  local copies, waits for them, and re-layouts: 58.8 us -> 36.3 us
  other arithmetic: 9.65 us -> 19.1 us
  Pallas kernels: 130 us -> 136 us
    all_gather x2 -> x0, blocking collectives: 164 us -> none  [the longest x1 100 us: routed(): places = lax.all_gather(place, axes, axis=0, tiled=True)]
    all_to_all x1, waiting for transfers between devices: 0.01 us -> 36.1 us  [shards(): lax.all_to_all(partial_value.astype(jnp.bfloat16), 'exp', split_axis=0, c...]
    unnamed x19 -> x27, local copies, waits for them, and re-layouts: 39 us -> 11.6 us
    all_to_all x1, waiting for transfers between devices: 5.6 us -> 0.01 us  [shards(): lax.all_to_all(total.reshape(count, H).astype(jnp.bfloat16), 'exp', split...]
    slice x1 -> x4, local copies, waits for them, and re-layouts: 0.22 us -> 5.51 us  [the longest x1 3.18 us: routed(): same = row[:, :, k:k + 1] == lanes]
  transfers between devices with their start and end apart: 4 -> 4, of which waited for: 2 -> 2; matrix products, arithmetic and copies ran while one was open for 13% -> 11% of each run, Pallas kernels for 0% -> 0%
where the time goes in v2:
time: 343 us; the launch traced here: 342 us
  Pallas kernels  136 us (40%)
  waiting for transfers between devices  87.5 us (26%)
  local copies, waits for them, and re-layouts  36.3 us (11%)
  matrix products  34.9 us (10%)
  other arithmetic  19.1 us (6%)
  starting transfers between devices  15.3 us (4%)
  between operations  13.7 us (4%)
    pallas_call x1, Pallas kernels, reduce_rows(): pl.pallas_call(reduce_kernel, out_shape=jax.ShapeDtypeStruct(stream.shape...  72.8 us
    all_gather x1, waiting for transfers between devices, shards(): q_all = lax.all_gather(query, 'exp', axis=0, tiled=True)  50.7 us
    pallas_call x1, Pallas kernels, gather_rows(): pl.pallas_call(gather_kernel, out_shape=(whole(mine), whole(note)), in_sp...  46.7 us
    all_to_all x1, waiting for transfers between devices, shards(): lax.all_to_all(partial_value.astype(jnp.bfloat16), 'exp', split_axis=0, c...  36.1 us
    pallas_call x1, Pallas kernels, run_experts(): pl.pallas_call(expert_kernel, out_shape=jax.ShapeDtypeStruct(rows.shape,...  16 us
    unnamed x27, local copies, waits for them, and re-layouts  11.6 us
    dot_general x1, matrix products, routed(): jnp.einsum('gtp,gpd->gtd', mixer, outs, preferred_element_type=jnp.float32)  8.17 us
    dot_general x1, matrix products, weighted_values(): jnp.einsum('qgjk,kgd->qgjd', weights, vh, preferred_element_type=jnp.floa...  8.16 us
  transfers between devices with their start and end apart: 4, of which 2 were waited for; matrix products, arithmetic and copies ran while one was open for 11% of the time, Pallas kernels for 0%

profile of v2, /device:TPU:0, one launch (start us, length us, event | category | flops | bytes accessed | tf_op | source)
XLA Modules:
  0.0 342.3 jit_solution(16387667430747266692)
XLA Ops:
  6.5 0.7 all-gather.2.cloned.1.call-update
  7.3 1.2 pad_maximum_fusion
  8.6 1.2 dynamic_slice.3
  9.8 0.7 fusion.69
  10.5 0.3 select_and_fusion
  10.8 50.7 %all-gather.2.cloned.1.call-done = bf16[512,2048]{1,0:T(8,128)(2,1)} async-done(((bf16[64,2048]{1,0:T(8,128)(2,1)}), bf16[512,2048]{1,0:T(8,128)(2,1)}) %all-gather.2.cloned.1.call-update) | async-done | bytes 2097168 | tf_op jit(solution)/shard_map/all_gather | solution.py:382
  61.5 2.9 copy.106
  64.4 5.9 %fusion = (f32[512,4,4]{0,2,1:T(4,128)S(1)}, f32[4,320,512,4]{2,1,3,0:T(8,128)}) fusion(pred[512,320]{0,1:T(8,128)(4,1)S(1)} %select_and_fusion, bf16[512,4,4,128]{0,3,2,1:T(8,128)(2,1)S(1)} %bitcast.96, bf16[320,4,128,1]{2,1,0,3:T(4,128)(2,1)S(1)} %bitcast.98), kind=kOutput, calls=%fused_computation.2 | convolution fusion | flops 678944768 | bytes 13107200 | tf_op jit(solution)/shard_map/qgjd,kgd->qgjk/dot_general | solution.py:46
  70.4 0.7 reshape.325
  71.1 3.3 all-to-all-start
  74.4 6.5 %fusion.1 = bf16[512,4,4]{0,2,1:T(4,128)(2,1)S(1)} fusion(f32[4,320,512,4]{2,1,3,0:T(8,128)} %get-tuple-element.26, f32[512,4,4]{0,2,1:T(4,128)S(1)} %get-tuple-element.25, pred[512,320]{0,1:T(8,128)(4,1)S(1)} %select_and_fusion), kind=kLoop, calls=%fused_computation.3 | loop fusion | flops 13099008 | bytes 10698752 | tf_op jit(solution)/shard_map/reduce_sum | solution.py:397
  81.1 0.7 reshape.327
  81.7 5.9 %all-to-all-start.2 = ((bf16[8,2,512]{2,1,0:T(2,128)(2,1)}), bf16[8,2,512]{2,1,0:T(2,128)(2,1)S(1)}, u32[]{:S(2)}, u32[]{:S(2)}) async-start(bf16[8,2,512]{2,1,0:T(2,128)(2,1)} %reshape.327), calls=%async_computation.2 | async-start | bytes 32768 | tf_op jit(solution)/shard_map/all_to_all | solution.py:409
  87.7 8.2 %convert_bitcast_fusion = bf16[512,4,4,128]{0,3,2,1:T(8,128)(2,1)} fusion(f32[4,320,512,4]{2,1,3,0:T(8,128)} %get-tuple-element.26, f32[512,4,4]{0,2,1:T(4,128)S(1)} %get-tuple-element.25, pred[512,320]{0,1:T(8,128)(4,1)S(1)} %select_and_fusion, bf16[320,4,128,1]{2,1,0,3:T(4,128)(2,1)S(1)} %bitcast.112), kind=kOutput, calls=%fused_computation.12 | convolution fusion | flops 685244416 | bytes 13107200 | tf_op jit(solution)/shard_map/qgjk,kgd->qgjd/dot_general | solution.py:53
  95.9 3.5 %copy.112 = bf16[512,4,4,128]{3,2,1,0:T(4,128)(2,1)S(1)} copy(bf16[512,4,4,128]{0,3,2,1:T(8,128)(2,1)} %convert_bitcast_fusion) | data formatting | bytes 4194304 | tf_op jit(solution)/shard_map/convert_element_type | solution.py:417
  99.3 2.9 convert_element_type.99
  102.2 6.0 %all-to-all-start.1 = ((bf16[8,64,2048]{2,1,0:T(8,128)(2,1)}), bf16[8,64,2048]{2,1,0:T(8,128)(2,1)S(1)}, u32[]{:S(2)}, u32[]{:S(2)}) async-start(bf16[8,64,2048]{2,1,0:T(8,128)(2,1)} %convert_element_type.99), calls=%async_computation.1 | async-start | bytes 4194304 | tf_op jit(solution)/shard_map/all_to_all | solution.py:416
  108.8 0.9 reduce-window.6
  109.7 0.2 slice_reduce_fusion
  110.3 0.7 fusion.53.note_ref
  111.5 2.6 mul.88
  114.1 4.9 %mul.89 = f32[8,64,2048]{2,1,0:T(8,128)} reshape(f32[8,64,16,128]{3,2,1,0:T(8,128)} %mul.88) | data formatting | bytes 8388608 | tf_op jit(solution)/shard_map/mul | solution.py:425
  119.0 36.1 %all-to-all-done.1 = bf16[8,64,2048]{2,1,0:T(8,128)(2,1)S(1)} async-done(((bf16[8,64,2048]{2,1,0:T(8,128)(2,1)}), bf16[8,64,2048]{2,1,0:T(8,128)(2,1)S(1)}, u32[]{:S(2)}, u32[]{:S(2)}) %all-to-all-start.1) | async-done | bytes 2097184 | tf_op jit(solution)/shard_map/all_to_all | solution.py:416
  155.1 2.8 multiply_reduce_fusion
  158.1 5.2 %fusion.16 = (f32[64]{0:T(128)S(1)}, bf16[64,2048]{1,0:T(8,128)(2,1)S(1)}) fusion(bf16[2048,2048]{1,0:T(8,128)(2,1)} %param.17, f32[64,2048]{1,0:T(8,128)S(1)} %multiply_reduce_fusion, f32[8,8,16,128]{3,2,1,0:T(8,128)S(1)} %bitcast.97, bf16[64,2048]{1,0:T(8,128)(2,1)S(1)} %copy-done), kind=kOutput, calls=%fused_computation.39 | convolution fusion | flops 537919424 | bytes 9961728 | tf_op jit(solution)/shard_map/dot_general | solution.py:428
  163.3 0.8 fusion.18.mine_ref
  164.2 46.7 %gather_rows.1 = (bf16[32,64,2048]{2,1,0:T(8,128)(2,1)}, bf16[32,64,128]{2,1,0:T(8,128)(2,1)}) custom-call(bf16[64,2048]{1,0:T(8,128)(2,1)} %fusion.18.mine_ref, bf16[64,128]{1,0:T(8,128)(2,1)} %fusion.53.note_ref), custom_call_target="tpu_custom_call" | custom-call | tf_op jit(solution)/shard_map/gather_rows/pallas_call | solution.py:177
  210.9 1.1 bitcast_convert_fusion
  212.2 1.9 fusion.87
  214.1 1.2 copy.144
  215.3 1.3 copy.152
  216.6 0.2 copy.150
  216.8 0.2 copy.148
  217.0 0.2 copy.146
  217.3 0.2 copy.154
  217.5 3.9 %fusion.12 = s32[2048,6]{1,0:T(8,128)S(1)} fusion(f32[2048,128]{1,0:T(8,128)S(1)} %bitcast_convert_fusion, s32[2048]{0:T(1024)S(1)} %fusion.55, s32[]{:T(128)S(6)} %mul.102), kind=kLoop, calls=%fused_computation.18 | loop fusion | flops 282624 | bytes 155652 | tf_op jit(solution)/shard_map/jit(_where)/select_n | solution.py:350
  221.4 3.2 fusion.86
  224.6 1.5 copy.143
  226.1 1.6 copy.151
  227.7 1.6 copy.149
  229.3 0.3 copy.147
  229.6 0.3 copy.145
  229.9 0.3 copy.153
  230.3 7.5 %convolution_convert_fusion.1 = bf16[8,128,2048]{2,1,0:T(8,128)(2,1)} fusion(bf16[8,256,2048]{2,1,0:T(8,128)(2,1)} %bitcast.95, s32[8,256]{1,0:T(8,128)S(1)} %bitcast.109, s32[8,256]{1,0:T(8,128)S(1)} %bitcast.101, s32[8,256]{1,0:T(8,128)S(1)} %bitcast.103, s32[8,256]{1,0:T(8,128)S(1)} %bitcast.105, s32[8,256]{1,0:T(8,128)S(1)} %bitcast.107, ...), kind=kOutput, calls=%fused_computation.9 | convolution fusion | flops 1079246848 | bytes 12632064 | tf_op jit(solution)/shard_map/gtp,gtd->gpd/dot_general | solution.py:360
  237.7 16.0 %run_experts.1 = bf16[8,4,32,2048]{3,2,1,0:T(8,128)(2,1)S(1)} custom-call(bf16[8,4,32,2048]{3,2,1,0:T(8,128)(2,1)} %bitcast.92, bf16[4,704,2048]{2,1,0:T(8,128)(2,1)} %bitcast.93, bf16[4,704,2048]{2,1,0:T(8,128)(2,1)} %bitcast.94, bf16[4,704,2048]{2,1,0:T(8,128)(2,1)} %down_ref.1), custom_call_target="tpu_custom_call" | custom-call | tf_op jit(solution)/shard_map/run_experts/pallas_call | solution.py:313
  253.8 8.2 %convolution_convert_fusion = bf16[8,256,2048]{2,1,0:T(8,128)(2,1)} fusion(bf16[8,128,2048]{2,1,0:T(8,128)(2,1)S(1)} %bitcast.88, bf16[8,256]{1,0:T(8,128)(2,1)S(1)} %bitcast.120, s32[8,256]{1,0:T(8,128)S(1)} %bitcast.110, bf16[8,256]{1,0:T(8,128)(2,1)S(1)} %bitcast.116, s32[8,256]{1,0:T(8,128)S(1)} %bitcast.102, bf16[8,256]{1,0:T(8,128)(2,1)S(1)} %bitcast.117, ...), kind=kOutput, calls=%fused_computation.5 | convolution fusion | flops 1081081856 | bytes 12656640 | tf_op jit(solution)/shard_map/gtp,gpd->gtd/dot_general | solution.py:363
  262.0 72.8 %reduce_rows.1 = bf16[64,2048]{1,0:T(8,128)(2,1)S(1)} custom-call(bf16[32,64,2048]{2,1,0:T(8,128)(2,1)} %bitcast.90, bf16[64,2048]{1,0:T(8,128)(2,1)S(1)} %get-tuple-element.28.stream_ref), custom_call_target="tpu_custom_call" | custom-call | tf_op jit(solution)/shard_map/reduce_rows/pallas_call | solution.py:275
  334.8 0.7 copy.173
  (42 shorter events, 2.2 us)
Async XLA Ops:
  6.5 55.0 %all-gather.2.cloned.1.call-start = ((), (), s32[]{:S(2)}) async-start(), calls=%async_computation.3 | async-start | bytes 2359296 | tf_op jit(solution)/shard_map/all_gather | solution.py:382
  71.1 10.7 %all-to-all-start = ((bf16[8,2,512]{2,1,0:T(2,128)(2,1)}), bf16[8,2,512]{2,1,0:T(2,128)(2,1)S(1)}, u32[]{:S(2)}, u32[]{:S(2)}) async-start(bf16[8,2,512]{2,1,0:T(2,128)(2,1)} %reshape.325), calls=%async_computation | async-start | bytes 32768 | tf_op jit(solution)/shard_map/all_to_all | solution.py:402
  81.7 20.4 %all-to-all-start.2 = ((bf16[8,2,512]{2,1,0:T(2,128)(2,1)}), bf16[8,2,512]{2,1,0:T(2,128)(2,1)S(1)}, u32[]{:S(2)}, u32[]{:S(2)}) async-start(bf16[8,2,512]{2,1,0:T(2,128)(2,1)} %reshape.327), calls=%async_computation.2 | async-start | bytes 32768 | tf_op jit(solution)/shard_map/all_to_all | solution.py:409
  95.8 12.3 %copy-start.1 = (s32[64,6]{0,1:T(8,128)S(1)}, s32[64,6]{0,1:T(8,128)}, u32[]{:S(2)}) copy-start(s32[64,6]{0,1:T(8,128)} %param.19) | copy-start | bytes 4612
  95.8 12.9 %copy-start.3 = (bf16[64,6]{0,1:T(8,128)(2,1)S(1)}, bf16[64,6]{0,1:T(8,128)(2,1)}, u32[]{:S(2)}) copy-start(bf16[64,6]{0,1:T(8,128)(2,1)} %param.20) | copy-start | bytes 2308
  102.2 52.9 %all-to-all-start.1 = ((bf16[8,64,2048]{2,1,0:T(8,128)(2,1)}), bf16[8,64,2048]{2,1,0:T(8,128)(2,1)S(1)}, u32[]{:S(2)}, u32[]{:S(2)}) async-start(bf16[8,64,2048]{2,1,0:T(8,128)(2,1)} %convert_element_type.99), calls=%async_computation.1 | async-start | bytes 4194304 | tf_op jit(solution)/shard_map/all_to_all | solution.py:416
  114.1 44.0 %copy-start = (bf16[64,2048]{1,0:T(8,128)(2,1)S(1)}, bf16[64,2048]{1,0:T(8,128)(2,1)}, u32[]{:S(2)}) copy-start(bf16[64,2048]{1,0:T(8,128)(2,1)} %param.16) | copy-start | bytes 786436
  158.1 5.2 %copy-start.2 = (f32[2048]{0:T(1024)S(1)}, f32[2048]{0:T(1024)}, u32[]{:S(2)}) copy-start(f32[2048]{0:T(1024)} %param.18) | copy-start | bytes 24580
Sparse Core Ops, SparseCore 0:
  9.5 51.9 all-gather.1

commit v3 on v2

--- a/solution.py
+++ b/solution.py
@@ -364,6 +364,165 @@
     return reduce_rows(part.astype(jnp.bfloat16).reshape(-1, tok_rows, D), stream)
 
 
+def attend_kernel(
+    q_ref, new_ref, cache_ref, lim_ref, out_ref,
+    q_all, keys, values, out_n, out_s, in_n, in_s, local_sem, send_sem, recv_sem,
+):
+    row, me = lax.axis_index("req"), lax.axis_index("exp")
+    f32 = jnp.float32
+    bits = jnp.bitwise_xor
+    greet([(row, bits(me, off)) for off in range(1, 8)])
+    tok, fresh = q_ref.shape[0], cache_ref.shape[1]
+    span = q_ref.shape[1] // KVH
+    kv_cols = KVH * HD
+
+    def pieces(head):
+        at = lambda first: pl.ds(pl.multiple_of(first + head * HD, HD), HD)
+        lot = me % 4
+        old, new = pl.ds(0, fresh), pl.ds(fresh, tok)
+        return (
+            (cache_ref.at[0, :, at(0)], keys.at[lot, old, :]),
+            (new_ref.at[:, at(0)], keys.at[lot, new, :]),
+            (cache_ref.at[0, :, at(kv_cols)], values.at[lot, old, :]),
+            (new_ref.at[:, at(kv_cols)], values.at[lot, new, :]),
+        )
+
+    def remote(src, dst, out_slot, in_slot, target):
+        return pltpu.make_async_remote_copy(
+            src_ref=src,
+            dst_ref=dst,
+            send_sem=send_sem.at[out_slot],
+            recv_sem=recv_sem.at[in_slot],
+            device_id=(row, target),
+            device_id_type=MESH,
+        )
+
+    def q_piece(head):
+        return q_ref.at[:, pl.ds(pl.multiple_of(head * span, span), span)]
+
+    sent, local = [], []
+    for off in (3, 2, 1):
+        other = bits(me, off)
+        for i, (src, dst) in enumerate(pieces(other % 4)):
+            n = 8 + off * 4 + i
+            sent.append(remote(src, dst, n, n, other))
+            sent[-1].start()
+    for off in (7, 6, 5, 4, 3, 2, 1):
+        other = bits(me, off)
+        sent.append(remote(q_piece(other % 4), q_all.at[me], off, off, other))
+        sent[-1].start()
+    for i, (src, dst) in enumerate((*pieces(me % 4), (q_piece(me % 4), q_all.at[me]))):
+        local.append(pltpu.make_async_copy(src, dst, local_sem.at[i]))
+        local[-1].start()
+    for copy in local:
+        copy.wait()
+    for off in (1, 2, 3):
+        lot = bits(me, off) % 4
+        old, new = pl.ds(0, fresh), pl.ds(fresh, tok)
+        lands = (keys.at[lot, old, :], keys.at[lot, new, :], values.at[lot, old, :], values.at[lot, new, :])
+        for i, dst in enumerate(lands):
+            n = 8 + off * 4 + i
+            remote(dst, dst, n, n, bits(me, off)).wait_recv()
+
+    def attend(owner):
+        q = q_all[owner]
+        group = H // KVH
+        stacked = jnp.concatenate([q[:, h * HD : (h + 1) * HD] for h in range(group)], 0)
+        k = keys[...].reshape(-1, HD)
+        v = values[...].reshape(-1, HD)
+        across = (((1,), (1,)), ((), ()))
+        scores = lax.dot_general(stacked, k, across, preferred_element_type=f32)
+        scores = scores * (1.0 / math.sqrt(HD))
+        here = owner * tok + lax.broadcasted_iota(jnp.int32, (group * tok, 1), 0) % tok
+        seen = lim_ref[...] <= here
+        masked = jnp.where(seen, scores, -1e30)
+        peak = jnp.max(masked, axis=1, keepdims=True)
+        expo = jnp.where(seen, jnp.exp(masked - peak), 0.0)
+        total = jnp.sum(expo, axis=1, keepdims=True)
+        numer = jnp.dot(expo.astype(jnp.bfloat16), v, preferred_element_type=f32)
+        lane = lax.broadcasted_iota(jnp.int32, (tok, 128), 1)
+        stats = jnp.zeros((tok, 128), f32)
+        parts = []
+        for h in range(group):
+            rows = slice(h * tok, (h + 1) * tok)
+            stats = jnp.where(lane == h, peak[rows], stats)
+            stats = jnp.where(lane == group + h, total[rows], stats)
+            parts.append(numer[rows])
+        return jnp.concatenate(parts, 1).astype(jnp.bfloat16), stats
+
+    @pl.loop(0, 7)
+    def _(step):
+        off = 7 - step
+        owner = bits(me, off)
+        remote(q_all.at[owner], q_all.at[owner], off, off, owner).wait_recv()
+        numer, stats = attend(owner)
+        out_n[step] = numer
+        out_s[step] = stats
+        remote(out_n.at[step], in_n.at[me], 24 + off, 24 + off, owner).start()
+        remote(out_s.at[step], in_s.at[me], 32 + off, 32 + off, owner).start()
+
+    numer, stats = attend(me)
+    in_n[me] = numer
+    in_s[me] = stats
+    for off in range(1, 8):
+        other = bits(me, off)
+        remote(in_n.at[other], in_n.at[other], 24 + off, 24 + off, other).wait_recv()
+        remote(in_s.at[other], in_s.at[other], 32 + off, 32 + off, other).wait_recv()
+    group = H // KVH
+    for head in range(KVH):
+        one, two = in_s[head], in_s[KVH + head]
+        for h in range(group):
+            p1, p2 = one[:, h : h + 1], two[:, h : h + 1]
+            top = jnp.maximum(p1, p2)
+            f1, f2 = jnp.exp(p1 - top), jnp.exp(p2 - top)
+            denom = f1 * one[:, group + h : group + h + 1] + f2 * two[:, group + h : group + h + 1]
+            cols = slice(h * HD, (h + 1) * HD)
+            numer = f1 * in_n[head, :, cols].astype(f32) + f2 * in_n[KVH + head, :, cols].astype(f32)
+            at = (head * group + h) * HD
+            out_ref[:, at : at + HD] = (numer / denom).astype(out_ref.dtype)
+    for copy in sent:
+        copy.wait_send()
+    for off in range(1, 8):
+        remote(out_n.at[7 - off], in_n.at[me], 24 + off, 24 + off, bits(me, off)).wait_send()
+        remote(out_s.at[7 - off], in_s.at[me], 32 + off, 32 + off, bits(me, off)).wait_send()
+
+
+def attend_rows(query, new_kv, cache_kv, cached_len):
+    tok, width = query.shape
+    piece = cache_kv.shape[1]
+    half = lax.axis_index("exp") // 4
+    length = lax.dynamic_index_in_dim(cached_len, lax.axis_index("req"), 0, keepdims=False)
+    holder = half * 4 + jnp.arange(4, dtype=jnp.int32)[:, None]
+    past = holder * piece + jnp.arange(piece, dtype=jnp.int32)[None, :]
+    past = jnp.where(past < length, -1, 1 << 20)
+    fresh = holder * tok + jnp.arange(tok, dtype=jnp.int32)[None, :]
+    lim = jnp.concatenate([past, fresh], 1).reshape(1, -1)
+    bf16, f32 = jnp.bfloat16, jnp.float32
+    span = width // KVH
+    return pl.pallas_call(
+        attend_kernel,
+        out_shape=jax.ShapeDtypeStruct(query.shape, query.dtype),
+        in_specs=[VMEM_SPEC] * 4,
+        out_specs=VMEM_SPEC,
+        scratch_shapes=[
+            pltpu.VMEM((8, tok, span), bf16),
+            pltpu.VMEM((4, piece + tok, HD), bf16),
+            pltpu.VMEM((4, piece + tok, HD), bf16),
+            pltpu.VMEM((7, tok, span), bf16),
+            pltpu.VMEM((7, tok, 128), f32),
+            pltpu.VMEM((8, tok, span), bf16),
+            pltpu.VMEM((8, tok, 128), f32),
+            pltpu.SemaphoreType.DMA((5,)),
+            pltpu.SemaphoreType.DMA((40,)),
+            pltpu.SemaphoreType.DMA((40,)),
+        ],
+        compiler_params=pltpu.CompilerParams(
+            collective_id=3, has_side_effects=True, vmem_limit_bytes=32 * 2**20
+        ),
+        name="attend_rows",
+    )(query, new_kv, cache_kv, lim)
+
+
 def shards(
     query, new_kv, cache_kv, cached_len, residual, w_out, gain, routes, gates, w_gate, w_up, w_down
 ):
@@ -376,54 +535,57 @@
     new_len = tok_rows * n_exp // req_here
     group_index = lax.axis_index("req")
     column = lax.axis_index("exp")
-    lens_group = lax.dynamic_slice_in_dim(cached_len, group_index * req_here, req_here)
-    keys_local = jnp.concatenate([cache_kv.reshape(req_here * piece_len, 2 * kv_cols), new_kv], 0)
-    block_rows = keys_local.shape[0]
-    q_all = lax.all_gather(query, "exp", axis=0, tiled=True)
-    count = q_all.shape[0]
-    seen = visibility(
-        jnp.arange(block_rows, dtype=jnp.int32),
-        column,
-        jnp.arange(count, dtype=jnp.int32),
-        lens_group,
-        piece_len,
-        tok_rows,
-        new_len,
-    )
-    scores = head_scores(q_all, keys_local[:, :kv_cols])
-    masked = jnp.where(seen[:, None, None, :], scores, -1e30)
-    peak = jnp.max(masked, axis=-1)
-    expo = jnp.where(seen[:, None, None, :], jnp.exp(masked - peak[..., None]), 0.0)
-    total = jnp.sum(expo, axis=-1)
-    partial_value = weighted_values(expo.astype(jnp.bfloat16), keys_local[:, kv_cols:]).reshape(
-        count, H * HD
-    )
-    peaks, totals, partials = (
-        lax.all_to_all(
-            peak.reshape(count, H).astype(jnp.bfloat16),
-            "exp",
-            split_axis=0,
-            concat_axis=0,
-            tiled=True,
-        ).astype(jnp.float32),
-        lax.all_to_all(
-            total.reshape(count, H).astype(jnp.bfloat16),
-            "exp",
-            split_axis=0,
-            concat_axis=0,
-            tiled=True,
-        ).astype(jnp.float32),
-        lax.all_to_all(
-            partial_value.astype(jnp.bfloat16), "exp", split_axis=0, concat_axis=0, tiled=True
-        ).astype(partial_value.dtype),
-    )
-    peaks = peaks.reshape(n_exp, tok_rows, H)
-    totals = totals.reshape(n_exp, tok_rows, H)
-    top = jnp.max(peaks, axis=0)
-    factor = jnp.exp(peaks - top[None])
-    denom = jnp.sum(factor * totals, axis=0)
-    numer = jnp.sum(factor[..., None] * partials.reshape(n_exp, tok_rows, H, HD), axis=0)
-    attended = (numer / denom[..., None]).reshape(tok_rows, H * HD).astype(jnp.bfloat16)
+    if (n_req, n_exp, tok_rows, req_here, piece_len) == (4, 8, 64, 1, 256):
+        attended = attend_rows(query, new_kv, cache_kv, cached_len)
+    else:
+        lens_group = lax.dynamic_slice_in_dim(cached_len, group_index * req_here, req_here)
+        keys_local = jnp.concatenate([cache_kv.reshape(req_here * piece_len, 2 * kv_cols), new_kv], 0)
+        block_rows = keys_local.shape[0]
+        q_all = lax.all_gather(query, "exp", axis=0, tiled=True)
+        count = q_all.shape[0]
+        seen = visibility(
+            jnp.arange(block_rows, dtype=jnp.int32),
+            column,
+            jnp.arange(count, dtype=jnp.int32),
+            lens_group,
+            piece_len,
+            tok_rows,
+            new_len,
+        )
+        scores = head_scores(q_all, keys_local[:, :kv_cols])
+        masked = jnp.where(seen[:, None, None, :], scores, -1e30)
+        peak = jnp.max(masked, axis=-1)
+        expo = jnp.where(seen[:, None, None, :], jnp.exp(masked - peak[..., None]), 0.0)
+        total = jnp.sum(expo, axis=-1)
+        partial_value = weighted_values(expo.astype(jnp.bfloat16), keys_local[:, kv_cols:]).reshape(
+            count, H * HD
+        )
+        peaks, totals, partials = (
+            lax.all_to_all(
+                peak.reshape(count, H).astype(jnp.bfloat16),
+                "exp",
+                split_axis=0,
+                concat_axis=0,
+                tiled=True,
+            ).astype(jnp.float32),
+            lax.all_to_all(
+                total.reshape(count, H).astype(jnp.bfloat16),
+                "exp",
+                split_axis=0,
+                concat_axis=0,
+                tiled=True,
+            ).astype(jnp.float32),
+            lax.all_to_all(
+                partial_value.astype(jnp.bfloat16), "exp", split_axis=0, concat_axis=0, tiled=True
+            ).astype(partial_value.dtype),
+        )
+        peaks = peaks.reshape(n_exp, tok_rows, H)
+        totals = totals.reshape(n_exp, tok_rows, H)
+        top = jnp.max(peaks, axis=0)
+        factor = jnp.exp(peaks - top[None])
+        denom = jnp.sum(factor * totals, axis=0)
+        numer = jnp.sum(factor[..., None] * partials.reshape(n_exp, tok_rows, H, HD), axis=0)
+        attended = (numer / denom[..., None]).reshape(tok_rows, H * HD).astype(jnp.bfloat16)
     stream = (
         residual.astype(jnp.float32) + jnp.dot(attended, w_out, preferred_element_type=jnp.float32)
     ).astype(jnp.bfloat16)
@@ -433,7 +595,7 @@
     ).astype(jnp.bfloat16)
     rows_here = w_gate.shape[0]
     devices = n_req * n_exp
-    if (n_req, n_exp, tok_rows) == (4, 8, 64):
+    if (n_req, n_exp, tok_rows, rows_here) == (4, 8, 64, 4):
         return routed(stream, normed, routes, gates, w_gate, w_up, w_down)
     flat = routes.reshape(-1)
     hits = (flat[:, None] == jnp.arange(EXPERTS, dtype=jnp.int32)[None, :]).astype(jnp.int32)

time: 343 us -> 226 us (0.66)
  waiting for transfers between devices: 87.5 us -> 0 us
  Pallas kernels: 136 us -> 172 us
  starting transfers between devices: 15.3 us -> 0 us
  matrix products: 34.9 us -> 21.1 us
  between operations: 13.7 us -> 0.11 us
  local copies, waits for them, and re-layouts: 36.3 us -> 23.1 us
  other arithmetic: 19.1 us -> 9.14 us
    all_gather x1 -> x0, waiting for transfers between devices: 50.7 us -> none  [shards(): q_all = lax.all_gather(query, 'exp', axis=0, tiled=True)]
    pallas_call x0 -> x1, Pallas kernels: none -> 38.7 us  [attend_rows(): pl.pallas_call(attend_kernel, out_shape=jax.ShapeDtypeStruct(query.shape,...]
    all_to_all x3 -> x0, waiting for transfers between devices: 36.1 us -> none  [the longest x1 36.1 us: shards(): lax.all_to_all(partial_value.astype(jnp.bfloat16), 'exp', split_axis=0, c...]
    all_to_all x3 -> x0, starting transfers between devices: 15.3 us -> none  [the longest x1 6 us: shards(): lax.all_to_all(partial_value.astype(jnp.bfloat16), 'exp', split_axis=0, c...]
    dot_general x2 -> x0, matrix products: 14.1 us -> none  [the longest x1 8.16 us: weighted_values(): jnp.einsum('qgjk,kgd->qgjd', weights, vh, preferred_element_type=jnp.floa...]
    reduce_sum x3 -> x0, other arithmetic: 9.34 us -> none  [the longest x1 6.5 us: shards(): total = jnp.sum(expo, axis=-1)]
    mul x2 -> x0, local copies, waits for them, and re-layouts: 7.51 us -> none  [shards(): factor[..., None] * partials.reshape(n_exp, tok_rows, H, HD)]
    convert_element_type x6 -> x0, local copies, waits for them, and re-layouts: 6.53 us -> none  [the longest x2 6.32 us: shards(): partial_value.astype(jnp.bfloat16)]
  transfers between devices with their start and end apart: 4 -> 0, of which waited for: 2 -> 0; matrix products, arithmetic and copies ran while one was open for 11% -> 0% of each run, Pallas kernels for 0% -> 0%
where the time goes in v3:
time: 226 us; the launch traced here: 225 us
  Pallas kernels  172 us (76%)
  local copies, waits for them, and re-layouts  23.1 us (10%)
  matrix products  21.1 us (9%)
  other arithmetic  9.14 us (4%)
    pallas_call x1, Pallas kernels, reduce_rows(): pl.pallas_call(reduce_kernel, out_shape=jax.ShapeDtypeStruct(stream.shape...  67.8 us
    pallas_call x1, Pallas kernels, gather_rows(): pl.pallas_call(gather_kernel, out_shape=(whole(mine), whole(note)), in_sp...  49.5 us
    pallas_call x1, Pallas kernels, attend_rows(): pl.pallas_call(attend_kernel, out_shape=jax.ShapeDtypeStruct(query.shape,...  38.7 us
    pallas_call x1, Pallas kernels, run_experts(): pl.pallas_call(expert_kernel, out_shape=jax.ShapeDtypeStruct(rows.shape,...  16 us
    unnamed x23, local copies, waits for them, and re-layouts  15.5 us
    dot_general x1, matrix products, routed(): jnp.einsum('gtp,gpd->gtd', mixer, outs, preferred_element_type=jnp.float32)  8.19 us
    dot_general x1, matrix products, routed(): jnp.einsum('gtp,gtd->gpd', pick, everyone, preferred_element_type=jnp.flo...  7.63 us
    dot_general x1, matrix products, shards(): jnp.dot(attended, w_out, preferred_element_type=jnp.float32)  5.24 us

profile of v3, /device:TPU:0, one launch (start us, length us, event | category | flops | bytes accessed | tf_op | source)
XLA Modules:
  0.0 225.4 jit_solution(11325012520522882126)
XLA Ops:
  0.0 1.2 dynamic_slice.4
  1.2 0.1 iota_add_fusion
  1.3 0.7 convert_element_type.53
  2.0 0.7 fusion.45
  2.7 0.1 reshape.120.lim_ref
  2.8 0.1 copy.67
  2.9 0.8 copy.68
  3.7 0.8 copy.64
  4.5 0.1 eq.125
  4.6 0.1 eq.121
  4.8 0.9 reduce-window.6
  5.7 0.2 slice_reduce_fusion
  6.0 0.1 fusion.33
  6.1 0.2 convert_element_type.56
  6.3 0.7 fusion.39.note_ref
  7.0 0.0 copy-start
  7.0 1.0 copy-done
  8.0 0.0 copy-start.1
  8.0 0.9 copy-done.1
  8.9 0.0 copy-start.2
  8.9 0.9 copy-done.2
  9.9 38.7 %attend_rows.1 = bf16[64,2048]{1,0:T(8,128)(2,1)S(1)} custom-call(bf16[64,2048]{1,0:T(8,128)(2,1)S(1)} %copy-done.1, bf16[64,1024]{1,0:T(8,128)(2,1)S(1)} %copy-done.2, bf16[1,256,1024]{2,1,0:T(8,128)(2,1)S(1)} %copy-done, s32[1,1280]{1,0:T(1,128)S(1)} %reshape.120.lim_ref), custom_call_target="tpu_custom_call" | custom-call | tf_op jit(solution)/shard_map/attend_rows/pallas_call | solution.py:502
  48.6 5.2 %fusion.8 = (f32[64]{0:T(128)S(1)}, bf16[64,2048]{1,0:T(8,128)(2,1)S(1)}) fusion(bf16[64,2048]{1,0:T(8,128)(2,1)S(1)} %attend_rows.1, bf16[2048,2048]{1,0:T(8,128)(2,1)} %param.17, bf16[64,2048]{1,0:T(8,128)(2,1)} %param.16), kind=kOutput, calls=%fused_computation.27 | convolution fusion | flops 537657280 | bytes 9175296 | tf_op jit(solution)/shard_map/dot_general | solution.py:590
  53.8 0.0 copy-done.3
  53.8 0.8 fusion.10.mine_ref
  54.7 49.5 %gather_rows.1 = (bf16[32,64,2048]{2,1,0:T(8,128)(2,1)}, bf16[32,64,128]{2,1,0:T(8,128)(2,1)}) custom-call(bf16[64,2048]{1,0:T(8,128)(2,1)} %fusion.10.mine_ref, bf16[64,128]{1,0:T(8,128)(2,1)} %fusion.39.note_ref), custom_call_target="tpu_custom_call" | custom-call | tf_op jit(solution)/shard_map/gather_rows/pallas_call | solution.py:177
  104.1 1.1 bitcast_convert_fusion
  105.3 0.2 slice.72
  105.5 3.9 %fusion.4 = s32[2048,6]{1,0:T(8,128)S(1)} fusion(f32[2048,128]{1,0:T(8,128)S(1)} %bitcast_convert_fusion, s32[2048]{0:T(1024)S(1)} %fusion.41, s32[]{:T(128)S(6)} %mul.86), kind=kLoop, calls=%fused_computation.9 | loop fusion | flops 282624 | bytes 155652 | tf_op jit(solution)/shard_map/jit(_where)/select_n | solution.py:350
  109.4 1.9 fusion.52
  111.3 1.2 copy.84
  112.5 1.3 copy.92
  113.8 0.2 copy.90
  114.0 0.2 copy.88
  114.2 0.2 copy.86
  114.5 0.2 copy.94
  114.7 3.4 %fusion.51 = (s32[8,256,1]{2,1,0:T(8,128)}, s32[8,256,1]{2,1,0:T(8,128)}, s32[8,256,1]{2,1,0:T(8,128)}, s32[8,256,1]{2,1,0:T(8,128)}, s32[8,256,1]{2,1,0:T(8,128)S(1)}, /*index=5*/s32[8,256,1]{2,1,0:T(8,128)S(1)}) fusion(s32[8,256,6]{2,1,0:T(8,128)S(1)} %bitcast.45), kind=kLoop, calls=%fused_computation.89 | loop fusion | bytes 98304 | tf_op jit(solution)/shard_map/slice | solution.py:356
  118.1 1.5 copy.83
  119.6 1.6 copy.91
  121.2 1.6 copy.89
  122.8 1.6 copy.87
  124.3 0.3 copy.85
  124.7 0.3 copy.93
  125.0 7.6 %convolution_convert_fusion.1 = bf16[8,128,2048]{2,1,0:T(8,128)(2,1)} fusion(bf16[8,256,2048]{2,1,0:T(8,128)(2,1)} %bitcast.51, s32[8,256]{1,0:T(8,128)S(1)} %bitcast.62, s32[8,256]{1,0:T(8,128)S(1)} %bitcast.54, s32[8,256]{1,0:T(8,128)S(1)} %bitcast.56, s32[8,256]{1,0:T(8,128)S(1)} %bitcast.58, s32[8,256]{1,0:T(8,128)S(1)} %bitcast.60, ...), kind=kOutput, calls=%fused_computation.1 | convolution fusion | flops 1079246848 | bytes 12632064 | tf_op jit(solution)/shard_map/gtp,gtd->gpd/dot_general | solution.py:360
  132.6 16.0 %run_experts.1 = bf16[8,4,32,2048]{3,2,1,0:T(8,128)(2,1)S(1)} custom-call(bf16[8,4,32,2048]{3,2,1,0:T(8,128)(2,1)} %bitcast.48, bf16[4,704,2048]{2,1,0:T(8,128)(2,1)} %bitcast.49, bf16[4,704,2048]{2,1,0:T(8,128)(2,1)} %bitcast.50, bf16[4,704,2048]{2,1,0:T(8,128)(2,1)} %down_ref.1), custom_call_target="tpu_custom_call" | custom-call | tf_op jit(solution)/shard_map/run_experts/pallas_call | solution.py:313
  148.7 8.2 %convolution_convert_fusion = bf16[8,256,2048]{2,1,0:T(8,128)(2,1)} fusion(bf16[8,128,2048]{2,1,0:T(8,128)(2,1)S(1)} %bitcast.44, bf16[8,256]{1,0:T(8,128)(2,1)S(1)} %bitcast.69, s32[8,256]{1,0:T(8,128)S(1)} %bitcast.63, bf16[8,256]{1,0:T(8,128)(2,1)S(1)} %bitcast.65, s32[8,256]{1,0:T(8,128)S(1)} %bitcast.55, bf16[8,256]{1,0:T(8,128)(2,1)S(1)} %bitcast.66, ...), kind=kOutput, calls=%fused_computation | convolution fusion | flops 1081081856 | bytes 12656640 | tf_op jit(solution)/shard_map/gtp,gpd->gtd/dot_general | solution.py:363
  156.8 67.8 %reduce_rows.1 = bf16[64,2048]{1,0:T(8,128)(2,1)S(1)} custom-call(bf16[32,64,2048]{2,1,0:T(8,128)(2,1)} %bitcast.46, bf16[64,2048]{1,0:T(8,128)(2,1)S(1)} %get-tuple-element.22.stream_ref), custom_call_target="tpu_custom_call" | custom-call | tf_op jit(solution)/shard_map/reduce_rows/pallas_call | solution.py:275
  224.7 0.7 copy.98
  (8 shorter events, 0.1 us)
Async XLA Ops:
  7.0 1.0 copy-start
  8.0 0.9 copy-start.1
  8.9 0.9 copy-start.2
  9.9 44.0 %copy-start.3 = (f32[2048]{0:T(1024)S(1)}, f32[2048]{0:T(1024)}, u32[]{:S(2)}) copy-start(f32[2048]{0:T(1024)} %param.18) | copy-start | bytes 24580

commit v4 on v3

--- a/solution.py
+++ b/solution.py
@@ -190,7 +190,7 @@
 
 
 def reduce_kernel(
-    part_ref, stream_ref, out_ref, in_c, in_b, in_a, in_z, sum_c, sum_b, sum_a, send_sem, recv_sem
+    mixer_ref, outs_ref, stream_ref, out_ref, out_c, in_c, in_b, in_a, in_z, sum_c, sum_b, sum_a, send_sem, recv_sem
 ):
     x, y, z, c = place_here()
     along, a_peer, b_peer, core_peer = partners(x, y, z, c)
@@ -230,17 +230,30 @@
 
     ks = (*OFFSETS, 0)
     order = [(da, db, k) for db in (1, 0) for da in (1, 0) for k in ks]
-    for da, db, k in order:
+    def mixed(b):
+        return jnp.dot(mixer_ref[b], outs_ref[b // 4], preferred_element_type=f32)
+
+    def give(da, db, k):
         xs, ys = stepped(x, y, 1 - c, da, db)
         i = label(da, db, k)
-        send(part_ref.at[block_of(xs, ys, (z + k) % 4, 1 - c)], in_c.at[i], i, core_peer)
-    for da, db, k in order:
+        out_c[i] = mixed(block_of(xs, ys, (z + k) % 4, 1 - c)).astype(out_c.dtype)
+        send(out_c.at[i], in_c.at[i], i, core_peer)
+
+    def take(da, db, k):
         i = label(da, db, k)
         xs, ys = stepped(x, y, c, da, db)
+        term = mixed(block_of(xs, ys, (z + k) % 4, c))
         arrived(in_c.at[i], i)
-        add(sum_c.at[i], part_ref.at[block_of(xs, ys, (z + k) % 4, c)], in_c.at[i])
+        sum_c[i] = (term + in_c[i].astype(f32)).astype(sum_c.dtype)
         if db == 1:
             send(sum_c.at[i], in_b.at[da * 4 + k], 16 + da * 4 + k, b_peer)
+
+    lag = 2
+    for n in range(len(order) + lag):
+        if n < len(order):
+            give(*order[n])
+        if n >= lag:
+            take(*order[n - lag])
     for da in (1, 0):
         for k in ks:
             j = da * 4 + k
@@ -269,15 +282,16 @@
         copy.wait_send()
 
 
-def reduce_rows(part, stream):
+def reduce_rows(mixer, outs, stream):
     rows, width = stream.shape
     space = lambda n: pltpu.VMEM((n, rows, width), jnp.bfloat16)
     return pl.pallas_call(
         reduce_kernel,
         out_shape=jax.ShapeDtypeStruct(stream.shape, stream.dtype),
-        in_specs=[VMEM_SPEC, VMEM_SPEC],
+        in_specs=[VMEM_SPEC] * 3,
         out_specs=VMEM_SPEC,
         scratch_shapes=[
+            space(16),
             space(16),
             space(8),
             space(4),
@@ -292,7 +306,57 @@
             collective_id=2, has_side_effects=True, vmem_limit_bytes=48 * 2**20
         ),
         name="reduce_rows",
-    )(part, stream)
+    )(mixer, outs, stream)
+
+
+def pick_kernel(all_ref, note_ref, first_ref, rows_ref, mixer_ref):
+    lots, tok, width = all_ref.shape
+    count = mixer_ref.shape[2]
+    here = count // 32
+    note = note_ref[...].reshape(lots * tok, 128).astype(jnp.float32)
+    first = first_ref[...].astype(jnp.float32)
+    lane = lax.broadcasted_iota(jnp.int32, (lots * tok, count), 1).astype(jnp.float32)
+    token = lax.broadcasted_iota(jnp.int32, (lots * tok, 1), 0)
+    lot = (token // tok).astype(jnp.float32)
+    pick = jnp.zeros((lots * tok, count), jnp.float32)
+    mixer = pick
+    for k in range(TOPK):
+        expert = note[:, k : k + 1] - first
+        row = expert * 32 + lot * CAP + note[:, TOPK + k : TOPK + k + 1]
+        same = lane == jnp.where((expert >= 0) & (expert < here), row, -1.0)
+        pick = jnp.where(same, 1.0, pick)
+        mixer = jnp.where(same, note[:, 2 * TOPK + k : 2 * TOPK + k + 1], mixer)
+    mixer_ref[...] = mixer.astype(mixer_ref.dtype).reshape(lots, tok, count)
+    rows = lax.dot_general(
+        pick.T.astype(jnp.bfloat16),
+        all_ref[...].reshape(lots * tok, width),
+        (((1,), (0,)), ((), ())),
+        preferred_element_type=jnp.float32,
+    )
+    rows_ref[...] = rows.astype(rows_ref.dtype).reshape(1, here, 32, width)
+
+
+def pick_rows(everyone, notes, first, here):
+    blocks, tok, width = everyone.shape
+    return pl.pallas_call(
+        pick_kernel,
+        out_shape=(
+            jax.ShapeDtypeStruct((blocks // 4, here, 32, width), everyone.dtype),
+            jax.ShapeDtypeStruct((blocks, tok, here * 32), everyone.dtype),
+        ),
+        grid=(blocks // 4,),
+        in_specs=[
+            pl.BlockSpec((4, tok, width), lambda g: (g, 0, 0)),
+            pl.BlockSpec((4, tok, 128), lambda g: (g, 0, 0)),
+            pl.BlockSpec((1, 1), lambda g: (0, 0)),
+        ],
+        out_specs=(
+            pl.BlockSpec((1, here, 32, width), lambda g: (g, 0, 0, 0)),
+            pl.BlockSpec((4, tok, here * 32), lambda g: (g, 0, 0)),
+        ),
+        compiler_params=pltpu.CompilerParams(vmem_limit_bytes=24 * 2**20),
+        name="pick_rows",
+    )(everyone, notes, first)
 
 
 def expert_kernel(rows_ref, gate_ref, up_ref, down_ref, out_ref):
@@ -338,30 +402,10 @@
     )
     note = jnp.pad(note, ((0, 0), (0, 128 - 3 * TOPK)))
     everyone, notes = gather_rows(normed, note)
-    tokens = everyone.shape[0] * tok_rows
-    everyone = everyone.reshape(8, tokens // 8, D)
-    notes = notes.reshape(tokens, 128).astype(jnp.float32)
-    places = (notes[:, :TOPK] * CAP + notes[:, TOPK : 2 * TOPK]).astype(jnp.int32)
-    shares = notes[:, 2 * TOPK : 3 * TOPK]
-    first = me * rows_here % EXPERTS * CAP
-    rel = places - first
-    lot = jnp.arange(tokens, dtype=jnp.int32)[:, None] // tok_rows % 4
-    row = rel // CAP * 32 + lot * CAP + rel % CAP
-    row = jnp.where((rel >= 0) & (rel < rows_here * CAP), row, -1).reshape(8, tokens // 8, TOPK)
-    shares = shares.reshape(8, tokens // 8, TOPK)
-    lanes = jnp.arange(rows_here * 32, dtype=jnp.int32)
-    pick = jnp.zeros((8, tokens // 8, rows_here * 32), jnp.float32)
-    mixer = pick
-    for k in range(TOPK):
-        same = row[:, :, k : k + 1] == lanes
-        pick = jnp.where(same, 1.0, pick)
-        mixer = jnp.where(same, shares[:, :, k : k + 1], mixer)
-    pick, mixer = pick.astype(jnp.bfloat16), mixer.astype(jnp.bfloat16)
-    rows = jnp.einsum("gtp,gtd->gpd", pick, everyone, preferred_element_type=jnp.float32)
-    rows = rows.astype(jnp.bfloat16).reshape(8, rows_here, 32, D)
+    first = (me * rows_here % EXPERTS).reshape(1, 1)
+    rows, mixer = pick_rows(everyone, notes, first, rows_here)
     outs = run_experts(rows, w_gate, w_up, w_down).reshape(8, rows_here * 32, D)
-    part = jnp.einsum("gtp,gpd->gtd", mixer, outs, preferred_element_type=jnp.float32)
-    return reduce_rows(part.astype(jnp.bfloat16).reshape(-1, tok_rows, D), stream)
+    return reduce_rows(mixer, outs, stream)
 
 
 def attend_kernel(

time: 226 us -> 200 us (0.88)
  matrix products: 21.1 us -> 5.08 us
  local copies, waits for them, and re-layouts: 23.1 us -> 13.6 us
  other arithmetic: 9.14 us -> 4.11 us
  Pallas kernels: 172 us -> 177 us
    dot_general x2 -> x0, matrix products: 15.8 us -> none  [the longest x1 8.19 us: routed(): jnp.einsum('gtp,gpd->gtd', mixer, outs, preferred_element_type=jnp.float32)]
    pallas_call x0 -> x1, Pallas kernels: none -> 7.5 us  [pick_rows(): pl.pallas_call(pick_kernel, out_shape=(jax.ShapeDtypeStruct((blocks // 4,...]
    slice x4 -> x1, local copies, waits for them, and re-layouts: 5.74 us -> 0.22 us  [the longest x1 3.41 us: routed(): same = row[:, :, k:k + 1] == lanes]
    unnamed x23 -> x17, local copies, waits for them, and re-layouts: 15.5 us -> 11.5 us
    select_n x1 -> x0, other arithmetic: 3.91 us -> none  [routed(): jnp.where((rel >= 0) & (rel < rows_here * CAP), row, -1)]
    pallas_call x1, Pallas kernels: 67.8 us -> 64.9 us  [reduce_rows(): pl.pallas_call(reduce_kernel, out_shape=jax.ShapeDtypeStruct(stream.shape...]
where the time goes in v4:
time: 200 us
  Pallas kernels  177 us (88%)
  local copies, waits for them, and re-layouts  13.6 us (7%)
  matrix products  5.08 us (3%)
  other arithmetic  4.11 us (2%)
    pallas_call x1, Pallas kernels, reduce_rows(): pl.pallas_call(reduce_kernel, out_shape=jax.ShapeDtypeStruct(stream.shape...  64.9 us
    pallas_call x1, Pallas kernels, gather_rows(): pl.pallas_call(gather_kernel, out_shape=(whole(mine), whole(note)), in_sp...  49.5 us
    pallas_call x1, Pallas kernels, attend_rows(): pl.pallas_call(attend_kernel, out_shape=jax.ShapeDtypeStruct(query.shape,...  38.7 us
    pallas_call x1, Pallas kernels, run_experts(): pl.pallas_call(expert_kernel, out_shape=jax.ShapeDtypeStruct(rows.shape,...  16.2 us
    unnamed x17, local copies, waits for them, and re-layouts  11.5 us
    pallas_call x1, Pallas kernels, pick_rows(): pl.pallas_call(pick_kernel, out_shape=(jax.ShapeDtypeStruct((blocks // 4,...  7.5 us
    dot_general x1, matrix products, shards(): jnp.dot(attended, w_out, preferred_element_type=jnp.float32)  5.08 us

profile of v4, /device:TPU:0, one launch (start us, length us, event | category | flops | bytes accessed | tf_op | source)
XLA Modules:
  0.0 199.6 jit_solution(4155563173224010874)
XLA Ops:
  0.0 1.2 dynamic_slice.4
  1.2 0.1 iota_add_fusion
  1.3 0.7 convert_element_type.32
  2.0 0.7 fusion.12
  2.7 0.1 reshape.49.lim_ref
  2.8 0.1 copy.28
  2.9 0.8 copy.29
  3.7 0.8 copy.25
  4.5 0.1 eq.31
  4.6 0.1 eq.27
  4.8 0.9 reduce-window.6
  5.7 0.2 slice_reduce_fusion
  6.0 0.1 fusion.5
  6.1 0.2 convert_element_type.35
  6.3 0.7 fusion.11.note_ref
  6.9 0.0 copy-start.3
  6.9 1.0 copy-done.3
  8.0 0.0 copy-start.4
  8.0 0.9 copy-done.4
  8.9 0.0 copy-start.5
  8.9 0.9 copy-done.5
  9.8 0.0 copy-start.6
  9.8 38.7 %attend_rows.1 = bf16[64,2048]{1,0:T(8,128)(2,1)S(1)} custom-call(bf16[64,2048]{1,0:T(8,128)(2,1)S(1)} %copy-done.4, bf16[64,1024]{1,0:T(8,128)(2,1)S(1)} %copy-done.5, bf16[1,256,1024]{2,1,0:T(8,128)(2,1)S(1)} %copy-done.3, s32[1,1280]{1,0:T(1,128)S(1)} %reshape.49.lim_ref), custom_call_target="tpu_custom_call" | custom-call | tf_op jit(solution)/shard_map/attend_rows/pallas_call | solution.py:546
  48.6 5.1 %fusion.1 = (f32[64]{0:T(128)S(1)}, bf16[64,2048]{1,0:T(8,128)(2,1)S(1)}) fusion(bf16[64,2048]{1,0:T(8,128)(2,1)S(1)} %attend_rows.1, bf16[2048,2048]{1,0:T(8,128)(2,1)} %param.17, bf16[64,2048]{1,0:T(8,128)(2,1)} %param.16), kind=kOutput, calls=%fused_computation.4 | convolution fusion | flops 537657280 | bytes 9175296 | tf_op jit(solution)/shard_map/dot_general | solution.py:634
  53.7 0.0 copy-done.6
  53.7 0.8 fusion.3.mine_ref
  54.5 49.5 %gather_rows.1 = (bf16[32,64,2048]{2,1,0:T(8,128)(2,1)}, bf16[32,64,128]{2,1,0:T(8,128)(2,1)}) custom-call(bf16[64,2048]{1,0:T(8,128)(2,1)} %fusion.3.mine_ref, bf16[64,128]{1,0:T(8,128)(2,1)} %fusion.11.note_ref), custom_call_target="tpu_custom_call" | custom-call | tf_op jit(solution)/shard_map/gather_rows/pallas_call | solution.py:177
  104.0 0.0 copy-start
  104.0 3.4 %copy-done = bf16[32,64,2048]{2,1,0:T(8,128)(2,1)S(1)} copy-done((bf16[32,64,2048]{2,1,0:T(8,128)(2,1)S(1)}, bf16[32,64,2048]{2,1,0:T(8,128)(2,1)}, u32[]{:S(2)}) %copy-start) | copy-done | bytes 8388632
  107.4 0.0 copy-start.2
  107.4 1.0 copy-done.2
  108.4 7.5 %pick_rows.1 = (bf16[8,4,32,2048]{3,2,1,0:T(8,128)(2,1)S(1)}, bf16[32,64,128]{2,1,0:T(8,128)(2,1)S(1)}) custom-call(bf16[32,64,2048]{2,1,0:T(8,128)(2,1)S(1)} %copy-done, bf16[32,64,128]{2,1,0:T(8,128)(2,1)S(1)} %copy-done.2, s32[1,1]{1,0:T(1,128)} %bitcast.2.first_ref), custom_call_target="tpu_custom_call" | custom-call | tf_op jit(solution)/shard_map/pick_rows/pallas_call | solution.py:341
  115.9 0.0 copy-start.1
  115.9 1.9 copy-done.1
  117.8 16.2 %run_experts.1 = bf16[8,4,32,2048]{3,2,1,0:T(8,128)(2,1)S(1)} custom-call(bf16[8,4,32,2048]{3,2,1,0:T(8,128)(2,1)} %copy-done.1, bf16[4,704,2048]{2,1,0:T(8,128)(2,1)} %bitcast.24, bf16[4,704,2048]{2,1,0:T(8,128)(2,1)} %bitcast.25, bf16[4,704,2048]{2,1,0:T(8,128)(2,1)} %down_ref.1), custom_call_target="tpu_custom_call" | custom-call | tf_op jit(solution)/shard_map/run_experts/pallas_call | solution.py:377
  134.1 64.9 %reduce_rows.1 = bf16[64,2048]{1,0:T(8,128)(2,1)S(1)} custom-call(bf16[32,64,128]{2,1,0:T(8,128)(2,1)S(1)} %get-tuple-element.11.mixer_ref, bf16[8,128,2048]{2,1,0:T(8,128)(2,1)S(1)} %bitcast.23, bf16[64,2048]{1,0:T(8,128)(2,1)S(1)} %get-tuple-element.14.stream_ref), custom_call_target="tpu_custom_call" | custom-call | tf_op jit(solution)/shard_map/reduce_rows/pallas_call | solution.py:288
  198.9 0.7 copy.33
  (6 shorter events, 0.1 us)
Async XLA Ops:
  6.9 1.0 copy-start.3
  8.0 0.9 copy-start.4
  8.9 0.9 copy-start.5
  9.8 43.8 %copy-start.6 = (f32[2048]{0:T(1024)S(1)}, f32[2048]{0:T(1024)}, u32[]{:S(2)}) copy-start(f32[2048]{0:T(1024)} %param.18) | copy-start | bytes 24580
  104.0 3.4 %copy-start = (bf16[32,64,2048]{2,1,0:T(8,128)(2,1)S(1)}, bf16[32,64,2048]{2,1,0:T(8,128)(2,1)}, u32[]{:S(2)}) copy-start(bf16[32,64,2048]{2,1,0:T(8,128)(2,1)} %get-tuple-element.9.all_ref) | copy-start | bytes 25165828
  107.4 1.0 copy-start.2
  115.9 1.9 copy-start.1

commit v5 on v4

--- a/solution.py
+++ b/solution.py
@@ -56,7 +56,7 @@
 MESH = pl.DeviceIdType.MESH
 VMEM_SPEC = pl.BlockSpec(memory_space=pltpu.VMEM)
 ANY_SPEC = pl.BlockSpec(memory_space=pl.ANY)
-OFFSETS = (1, 3, 2)
+OFFSETS = (2, 1, 3)
 
 
 def place_here():
@@ -248,7 +248,7 @@
         if db == 1:
             send(sum_c.at[i], in_b.at[da * 4 + k], 16 + da * 4 + k, b_peer)
 
-    lag = 2
+    lag = 1
     for n in range(len(order) + lag):
         if n < len(order):
             give(*order[n])

time: 200 us -> 202 us (1.010); the launches traced: 200 us -> 199 us
    pallas_call x1, Pallas kernels: 64.9 us -> 57.9 us  [reduce_rows(): pl.pallas_call(reduce_kernel, out_shape=jax.ShapeDtypeStruct(stream.shape...]
    pallas_call x1, Pallas kernels: 49.5 us -> 55.4 us  [gather_rows(): pl.pallas_call(gather_kernel, out_shape=(whole(mine), whole(note)), in_sp...]
where the time goes in v5:
time: 202 us; the launch traced here: 199 us
  Pallas kernels  176 us (87%)
  local copies, waits for them, and re-layouts  13.6 us (7%)
  matrix products  5.08 us (3%)
  other arithmetic  4.11 us (2%)
    pallas_call x1, Pallas kernels, reduce_rows(): pl.pallas_call(reduce_kernel, out_shape=jax.ShapeDtypeStruct(stream.shape...  57.9 us
    pallas_call x1, Pallas kernels, gather_rows(): pl.pallas_call(gather_kernel, out_shape=(whole(mine), whole(note)), in_sp...  55.4 us
    pallas_call x1, Pallas kernels, attend_rows(): pl.pallas_call(attend_kernel, out_shape=jax.ShapeDtypeStruct(query.shape,...  38.7 us
    pallas_call x1, Pallas kernels, run_experts(): pl.pallas_call(expert_kernel, out_shape=jax.ShapeDtypeStruct(rows.shape,...  16.2 us
    unnamed x17, local copies, waits for them, and re-layouts  11.5 us
    pallas_call x1, Pallas kernels, pick_rows(): pl.pallas_call(pick_kernel, out_shape=(jax.ShapeDtypeStruct((blocks // 4,...  7.5 us
    dot_general x1, matrix products, shards(): jnp.dot(attended, w_out, preferred_element_type=jnp.float32)  5.08 us

profile of v5, /device:TPU:0, one launch (start us, length us, event | category | flops | bytes accessed | tf_op | source)
XLA Modules:
  0.0 198.7 jit_solution(778915380099699491)
XLA Ops:
  0.0 1.2 dynamic_slice.4
  1.2 0.1 iota_add_fusion
  1.3 0.7 convert_element_type.32
  2.0 0.7 fusion.12
  2.7 0.1 reshape.49.lim_ref
  2.8 0.1 copy.28
  2.9 0.8 copy.29
  3.7 0.8 copy.25
  4.5 0.1 eq.31
  4.6 0.1 eq.27
  4.8 0.9 reduce-window.6
  5.7 0.2 slice_reduce_fusion
  6.0 0.1 fusion.5
  6.1 0.2 convert_element_type.35
  6.3 0.7 fusion.11.note_ref
  6.9 0.0 copy-start.3
  6.9 1.0 copy-done.3
  8.0 0.0 copy-start.4
  8.0 0.9 copy-done.4
  8.9 0.0 copy-start.5
  8.9 0.9 copy-done.5
  9.8 0.0 copy-start.6
  9.8 38.7 %attend_rows.1 = bf16[64,2048]{1,0:T(8,128)(2,1)S(1)} custom-call(bf16[64,2048]{1,0:T(8,128)(2,1)S(1)} %copy-done.4, bf16[64,1024]{1,0:T(8,128)(2,1)S(1)} %copy-done.5, bf16[1,256,1024]{2,1,0:T(8,128)(2,1)S(1)} %copy-done.3, s32[1,1280]{1,0:T(1,128)S(1)} %reshape.49.lim_ref), custom_call_target="tpu_custom_call" | custom-call | tf_op jit(solution)/shard_map/attend_rows/pallas_call | solution.py:546
  48.6 5.1 %fusion.1 = (f32[64]{0:T(128)S(1)}, bf16[64,2048]{1,0:T(8,128)(2,1)S(1)}) fusion(bf16[64,2048]{1,0:T(8,128)(2,1)S(1)} %attend_rows.1, bf16[2048,2048]{1,0:T(8,128)(2,1)} %param.17, bf16[64,2048]{1,0:T(8,128)(2,1)} %param.16), kind=kOutput, calls=%fused_computation.4 | convolution fusion | flops 537657280 | bytes 9175296 | tf_op jit(solution)/shard_map/dot_general | solution.py:634
  53.7 0.0 copy-done.6
  53.7 0.8 fusion.3.mine_ref
  54.5 55.4 %gather_rows.1 = (bf16[32,64,2048]{2,1,0:T(8,128)(2,1)}, bf16[32,64,128]{2,1,0:T(8,128)(2,1)}) custom-call(bf16[64,2048]{1,0:T(8,128)(2,1)} %fusion.3.mine_ref, bf16[64,128]{1,0:T(8,128)(2,1)} %fusion.11.note_ref), custom_call_target="tpu_custom_call" | custom-call | tf_op jit(solution)/shard_map/gather_rows/pallas_call | solution.py:177
  109.9 0.0 copy-start
  110.0 3.4 %copy-done = bf16[32,64,2048]{2,1,0:T(8,128)(2,1)S(1)} copy-done((bf16[32,64,2048]{2,1,0:T(8,128)(2,1)S(1)}, bf16[32,64,2048]{2,1,0:T(8,128)(2,1)}, u32[]{:S(2)}) %copy-start) | copy-done | bytes 8388632
  113.3 0.0 copy-start.2
  113.3 1.0 copy-done.2
  114.4 7.5 %pick_rows.1 = (bf16[8,4,32,2048]{3,2,1,0:T(8,128)(2,1)S(1)}, bf16[32,64,128]{2,1,0:T(8,128)(2,1)S(1)}) custom-call(bf16[32,64,2048]{2,1,0:T(8,128)(2,1)S(1)} %copy-done, bf16[32,64,128]{2,1,0:T(8,128)(2,1)S(1)} %copy-done.2, s32[1,1]{1,0:T(1,128)} %bitcast.2.first_ref), custom_call_target="tpu_custom_call" | custom-call | tf_op jit(solution)/shard_map/pick_rows/pallas_call | solution.py:341
  121.9 0.0 copy-start.1
  121.9 1.9 copy-done.1
  123.8 16.2 %run_experts.1 = bf16[8,4,32,2048]{3,2,1,0:T(8,128)(2,1)S(1)} custom-call(bf16[8,4,32,2048]{3,2,1,0:T(8,128)(2,1)} %copy-done.1, bf16[4,704,2048]{2,1,0:T(8,128)(2,1)} %bitcast.24, bf16[4,704,2048]{2,1,0:T(8,128)(2,1)} %bitcast.25, bf16[4,704,2048]{2,1,0:T(8,128)(2,1)} %down_ref.1), custom_call_target="tpu_custom_call" | custom-call | tf_op jit(solution)/shard_map/run_experts/pallas_call | solution.py:377
  140.0 57.9 %reduce_rows.1 = bf16[64,2048]{1,0:T(8,128)(2,1)S(1)} custom-call(bf16[32,64,128]{2,1,0:T(8,128)(2,1)S(1)} %get-tuple-element.11.mixer_ref, bf16[8,128,2048]{2,1,0:T(8,128)(2,1)S(1)} %bitcast.23, bf16[64,2048]{1,0:T(8,128)(2,1)S(1)} %get-tuple-element.14.stream_ref), custom_call_target="tpu_custom_call" | custom-call | tf_op jit(solution)/shard_map/reduce_rows/pallas_call | solution.py:288
  198.0 0.7 copy.33
  (6 shorter events, 0.1 us)
Async XLA Ops:
  6.9 1.0 copy-start.3
  8.0 0.9 copy-start.4
  8.9 0.9 copy-start.5
  9.8 43.8 %copy-start.6 = (f32[2048]{0:T(1024)S(1)}, f32[2048]{0:T(1024)}, u32[]{:S(2)}) copy-start(f32[2048]{0:T(1024)} %param.18) | copy-start | bytes 24580
  109.9 3.4 %copy-start = (bf16[32,64,2048]{2,1,0:T(8,128)(2,1)S(1)}, bf16[32,64,2048]{2,1,0:T(8,128)(2,1)}, u32[]{:S(2)}) copy-start(bf16[32,64,2048]{2,1,0:T(8,128)(2,1)} %get-tuple-element.9.all_ref) | copy-start | bytes 25165828
  113.3 1.0 copy-start.2
  121.9 1.9 copy-start.1
